TPU v7x, 128 devices: a whole 4x4x4 slice. The times are simulated.
128 devices in a mesh: ang: 32 (over z, y, x_hi), pos: 4 (over x_lo, core).
Axes of the slice: x: 4 (x_hi: 2, x_lo: 2; x = x_hi * 2 + x_lo), y: 4, z: 4, core: 2. Of those that a mesh axis runs over, the one named last changes fastest.
Arguments:
- volume: bfloat16 [2, 256, 32768], P(None, 'ang', 'pos'), may hold values from -6 to 6
- radon_tiles: bfloat16 [128, 64, 256], replicated, may hold values from -0.375 to 0.375
- tile_blocks: int32 [128, 32, 4], replicated, may hold values from 0 to 511
- probe_field: bfloat16 [2, 256, 256], replicated, may hold values from -6 to 6
- amplitudes: bfloat16 [128, 16, 256, 256], P('ang', 'pos'), may hold values from 0.099609375 to 3
- offsets: int32 [128, 16], P('ang', 'pos'), may hold values from 0 to 2047, as said below
- counts: int32 [128, 4], P('ang', 'pos'), may hold values from 1 to 4, 12 in all within a row
Outputs:
- new_volume: float32 [2, 256, 32768], P(None, 'ang', 'pos')
- proj_grad: float32 [2, 256, 128, 2048], P(None, None, 'ang', 'pos')
Inputs may be any that keep to these rules, and one draw needn't show every extreme that they name: Each position lies in the tile of the device that holds its slot: 512 * (q // 4) <= offsets[a, q] < 512 * (q // 4 + 1). Every row of counts has an entry equal to 4.
All inputs are finite; a program needn't handle non-finite values. No bound on the sum of `counts` on one device may be relied on, other than what follows from the above.
Results may differ from a plain program's by a relative error of at most 0.0062.
Values may be sent and summed in bfloat16 or wider, within the bound.
A program may use at most 192 MiB of HBM per device.

v0:
```python
import math

import jax
import jax.numpy as jnp
from jax import lax
from jax.sharding import PartitionSpec as P

step_size = 0.1


def from_behind(block, axis, distance):
    devices = range(lax.axis_size(axis))
    route = [((i - distance) % len(devices), i) for i in devices]
    return lax.ppermute(block, axis, route)


def dft_tables(width):
    index = jnp.arange(width, dtype=jnp.int32)
    phase = index[:, None] * index[None, :] % width
    turn = 2.0 * math.pi / width * phase.astype(jnp.float32)
    cosine = (jnp.cos(turn) / math.sqrt(width)).astype(jnp.bfloat16)
    sine_neg = (-jnp.sin(turn) / math.sqrt(width)).astype(jnp.bfloat16)
    return (cosine, sine_neg)


def left_mul(table, field):
    return jnp.einsum("zy,qyu->qzu", table, field, preferred_element_type=jnp.float32)


def right_mul(field, table):
    return jnp.einsum("qzy,yu->qzu", field, table, preferred_element_type=jnp.float32)


def exit_gradient(patches, probe_field, amplitude_rows, live_mask, cosine, sine_neg):
    probe_re = probe_field[0].astype(jnp.float32)
    probe_im = probe_field[1].astype(jnp.float32)
    patch_re = patches[:, 0].astype(jnp.float32)
    patch_im = patches[:, 1].astype(jnp.float32)
    wave_re = (probe_re * patch_re - probe_im * patch_im).astype(jnp.bfloat16)
    wave_im = (probe_re * patch_im + probe_im * patch_re).astype(jnp.bfloat16)
    half_re = (left_mul(cosine, wave_re) - left_mul(sine_neg, wave_im)).astype(jnp.bfloat16)
    half_im = (left_mul(cosine, wave_im) + left_mul(sine_neg, wave_re)).astype(jnp.bfloat16)
    far_re = right_mul(half_re, cosine) - right_mul(half_im, sine_neg)
    far_im = right_mul(half_re, sine_neg) + right_mul(half_im, cosine)
    modulus = jnp.sqrt(far_re * far_re + far_im * far_im)
    factor = amplitude_rows.astype(jnp.float32) / jnp.maximum(modulus, 1.0) - 1.0
    delta_re = (far_re * factor).astype(jnp.bfloat16)
    delta_im = (far_im * factor).astype(jnp.bfloat16)
    back_re = (left_mul(cosine, delta_re) + left_mul(sine_neg, delta_im)).astype(jnp.bfloat16)
    back_im = (left_mul(cosine, delta_im) - left_mul(sine_neg, delta_re)).astype(jnp.bfloat16)
    near_re = right_mul(back_re, cosine) + right_mul(back_im, sine_neg)
    near_im = right_mul(back_im, cosine) - right_mul(back_re, sine_neg)
    scale_mask = live_mask[:, None, None]
    grad_re = (probe_re * near_re + probe_im * near_im) * scale_mask
    grad_im = (probe_re * near_im - probe_im * near_re) * scale_mask
    return jnp.stack([grad_re, grad_im], axis=1)


def selector(block_ids, block_total):
    flat_ids = block_ids.reshape(-1)
    return flat_ids[:, None] == jnp.arange(block_total, dtype=jnp.int32)[None, :]


def project(volume_part, block_ids, radon_tiles):
    block_size = radon_tiles.shape[1]
    slab_count = volume_part.shape[1]
    angle_count = block_ids.shape[0]
    det_count = block_ids.shape[1]
    feeds = block_ids.shape[2]
    block_total = volume_part.shape[2] // block_size
    blocks = volume_part.reshape(2, slab_count, block_total, block_size)
    choose = selector(block_ids, block_total).astype(jnp.bfloat16)
    picked = jnp.einsum("rk,cskx->csrx", choose, blocks, preferred_element_type=jnp.float32).astype(
        jnp.bfloat16
    )
    picked = picked.reshape(2, slab_count, angle_count, det_count, feeds * block_size)
    products = jnp.einsum(
        "csaux,amx->csaum", picked, radon_tiles, preferred_element_type=jnp.float32
    )
    return products.reshape(2, slab_count, angle_count, det_count * block_size)


def back_project(grad_part, block_ids, radon_tiles, coef_count):
    block_size = radon_tiles.shape[1]
    slab_count = grad_part.shape[1]
    angle_count = block_ids.shape[0]
    det_count = block_ids.shape[1]
    feeds = block_ids.shape[2]
    block_total = coef_count // block_size
    grad_blocks = grad_part.reshape(2, slab_count, angle_count, det_count, block_size)
    contrib = jnp.einsum(
        "csaum,amx->csaux", grad_blocks, radon_tiles, preferred_element_type=jnp.float32
    )
    contrib = contrib.reshape(2, slab_count, angle_count * det_count * feeds, block_size)
    choose = selector(block_ids, block_total).astype(jnp.float32)
    summed = jnp.einsum("rk,csrx->cskx", choose, contrib, precision=lax.Precision.HIGHEST)
    return summed.reshape(2, slab_count, coef_count)


def on_device(volume, radon_tiles, tile_blocks, probe_field, amplitudes, offsets, counts):
    n_pos = lax.axis_size("pos")
    pos_index = lax.axis_index("pos")
    block_size = radon_tiles.shape[1]
    own_blocks = tile_blocks.shape[1] // n_pos
    tile_width = own_blocks * block_size
    whole_volume = lax.all_gather(volume, "pos", axis=2, tiled=True)
    own_ids = lax.dynamic_slice_in_dim(tile_blocks, pos_index * own_blocks, own_blocks, 1)
    sinogram = project(whole_volume, own_ids, radon_tiles).astype(jnp.bfloat16)
    angle_major = lax.all_to_all(sinogram, "ang", split_axis=2, concat_axis=1, tiled=True)
    nextdoor = from_behind(angle_major, "pos", -1)
    extended = jnp.concatenate([angle_major, nextdoor], axis=3)
    probe_width = probe_field.shape[1]
    cosine, sine_neg = dft_tables(probe_width)
    all_slices = angle_major.shape[1]
    slot_count = offsets.shape[1]
    per_angle = []
    for angle_idx in range(angle_major.shape[2]):
        starts = offsets[angle_idx] - pos_index * tile_width
        extended_angle = extended[:, :, angle_idx, :]
        patches = jnp.stack(
            [
                lax.dynamic_slice_in_dim(extended_angle, starts[slot], probe_width, 2)
                for slot in range(slot_count)
            ],
            axis=0,
        )
        live_mask = (jnp.arange(slot_count, dtype=jnp.int32) < counts[angle_idx, 0]).astype(
            jnp.float32
        )
        patch_grads = exit_gradient(
            patches, probe_field, amplitudes[angle_idx], live_mask, cosine, sine_neg
        )
        summed = jnp.zeros((2, all_slices, 2 * tile_width), jnp.float32)
        for slot in range(slot_count):
            current = lax.dynamic_slice_in_dim(summed, starts[slot], probe_width, 2)
            summed = lax.dynamic_update_slice_in_dim(
                summed, current + patch_grads[slot], starts[slot], 2
            )
        per_angle.append(summed)
    spread = jnp.stack(per_angle, axis=2)
    spill_over = from_behind(spread[..., tile_width:], "pos", 1)
    proj_grad = spread[..., :tile_width] + spill_over
    grad_rounded = proj_grad.astype(jnp.bfloat16)
    slice_major = lax.all_to_all(grad_rounded, "ang", split_axis=1, concat_axis=2, tiled=True)
    partial_grad = back_project(slice_major, own_ids, radon_tiles, whole_volume.shape[2])
    object_grad = lax.psum_scatter(partial_grad, "pos", scatter_dimension=2, tiled=True)
    new_volume = volume.astype(jnp.float32) + step_size * object_grad
    return (new_volume, proj_grad)


def solution(mesh):
    in_specs = (
        P(None, "ang", "pos"),
        P(),
        P(),
        P(),
        P("ang", "pos", None, None),
        P("ang", "pos"),
        P("ang", "pos"),
    )
    out_specs = (P(None, "ang", "pos"), P(None, None, "ang", "pos"))
    return jax.shard_map(
        on_device, mesh=mesh, in_specs=in_specs, out_specs=out_specs, check_vma=False
    )
```

profile of v0, /device:TPU:1, one launch (start us, length us, event | category | flops | bytes accessed | tf_op | source)
XLA Modules:
  0.0 573.8 jit_solution(333616147310333617)
XLA Ops:
  8.6 25.4 %all-gather.2.cloned.1.call-done = bf16[2,8,32768]{2,1,0:T(8,128)(2,1)} async-done(((bf16[2,8,8192]{2,1,0:T(8,128)(2,1)}), bf16[2,8,32768]{2,1,0:T(8,128)(2,1)}) %all-gather.2.cloned.1.call-update) | async-done | bytes 1048592 | tf_op jit(solution)/shard_map/all_gather | solution.py:106
  34.0 3.0 reshape.147
  37.0 7.4 %convert_bitcast_fusion = bf16[2,8,4096,64]{2,3,1,0:T(8,128)(2,1)} fusion(bf16[2,8,512,64]{3,2,1,0:T(8,128)(2,1)S(1)} %reshape.147, s32[4096]{0:T(1024)S(1)} %eq.10), kind=kOutput, calls=%fused_computation.4 | convolution fusion | flops 4301258752 | bytes 9453568 | tf_op jit(solution)/shard_map/rk,cskx->csrx/dot_general | solution.py:73
  44.4 15.5 %copy.343 = bf16[2,8,4096,64]{3,2,1,0:T(8,128)(2,1)} copy(bf16[2,8,4096,64]{2,3,1,0:T(8,128)(2,1)} %convert_bitcast_fusion) | data formatting | bytes 16777216 | tf_op jit(solution)/shard_map/convert_element_type | solution.py:73
  59.9 22.8 %reshape.148 = bf16[2,8,128,8,256]{4,3,2,1,0:T(8,128)(2,1)} reshape(bf16[2,8,4096,64]{3,2,1,0:T(8,128)(2,1)} %copy.343) | data formatting | bytes 16777216 | tf_op jit(solution)/shard_map/reshape | solution.py:76
  82.7 8.9 %convert_bitcast_fusion.1 = bf16[2,8,128,8,64]{4,3,1,0,2:T(8,128)(2,1)} fusion(bf16[128,64,256]{2,1,0:T(8,128)(2,1)} %param.8, bf16[2,8,128,8,256]{4,3,2,1,0:T(8,128)(2,1)} %reshape.148), kind=kOutput, calls=%fused_computation.19 | convolution fusion | flops 537919488 | bytes 14680064 | tf_op jit(solution)/shard_map/csaux,amx->csaum/dot_general | solution.py:77
  91.6 5.6 copy.345
  97.3 2.9 copy.346
  100.2 38.9 %all_to_all.33 = bf16[2,8,128,512]{3,1,0,2:T(8,128)(2,1)S(1)} all-to-all(bf16[2,8,128,512]{3,1,0,2:T(8,128)(2,1)} %copy.346), channel_id=1, replica_groups=mesh['ang'=32,'pos'=4] {'ang'}, dimensions={2} | all-to-all | bytes 4194304 | tf_op jit(solution)/shard_map/all_to_all | solution.py:109
  139.3 1.8 collective-permute-start
  175.8 1.7 fusion.70
  189.9 1.6 fusion.40
  203.2 1.8 fusion.193
  215.6 1.4 convolution_add_fusion.10
  223.4 5.4 multiply_convert_fusion.7
  240.2 1.7 fusion.45
  253.2 1.4 fusion.169
  266.0 1.7 convolution_add_fusion.4
  268.9 4.0 multiply_bitcast_fusion.6
  274.7 1.6 broadcast.44.clone.3
  276.3 3.9 dynamic_update_slice.52
  280.2 2.3 fusion.107
  282.5 3.9 dynamic_update_slice.53
  286.4 2.3 fusion.102
  288.7 3.9 dynamic_update_slice.54
  292.6 2.5 fusion.119
  295.9 1.6 broadcast.44.clone.2
  297.5 3.9 dynamic_update_slice.56
  301.5 2.3 fusion.99
  303.8 3.9 dynamic_update_slice.57
  307.7 2.3 fusion.94
  310.0 3.9 dynamic_update_slice.58
  313.8 2.4 fusion.116
  317.1 1.6 broadcast.44.clone.1
  318.7 3.9 dynamic_update_slice.60
  322.6 2.2 fusion.91
  324.8 3.9 dynamic_update_slice.61
  328.8 2.2 fusion.86
  331.0 4.0 dynamic_update_slice.62
  335.0 2.3 fusion.113
  337.2 1.6 broadcast.44.clone
  338.8 3.8 dynamic_update_slice.64
  343.9 3.8 dynamic_update_slice.65
  349.0 3.8 dynamic_update_slice.66
  352.8 2.2 fusion.110
  355.0 3.9 dynamic_update_slice.55
  359.0 3.8 dynamic_update_slice.59
  362.8 4.0 dynamic_update_slice.63
  366.8 4.5 dynamic_update_slice.67
  371.3 3.3 pad_maximum_fusion
  375.7 45.4 %collective-permute-done.1 = f32[2,256,4,512]{3,1,0,2:T(8,128)S(1)} collective-permute-done((f32[2,256,4,512]{3,1,0,2:T(8,128)S(1)}, f32[2,256,4,512]{3,1,0,2:T(8,128)S(1)}, u32[]{:S(2)}, u32[]{:S(2)}) %collective-permute-start.1) | collective-permute-done | bytes 4194336 | tf_op jit(solution)/shard_map/ppermute | solution.py:14
  421.1 3.1 fusion.561
  424.2 2.2 copy.422
  426.4 31.9 %all_to_all.34 = bf16[2,256,4,512]{3,0,2,1:T(2,128)(2,1)S(1)} all-to-all(bf16[2,256,4,512]{3,0,2,1:T(2,128)(2,1)S(1)} %copy.422), channel_id=1, replica_groups=mesh['ang'=32,'pos'=4] {'ang'}, dimensions={1} | all-to-all | bytes 4194304 | tf_op jit(solution)/shard_map/all_to_all | solution.py:144
  459.2 3.6 reshape.149
  462.8 5.8 %convolution_bitcast_fusion = f32[2,8,128,8,256]{4,3,1,0,2:T(8,128)S(1)} fusion(bf16[128,64,256]{2,1,0:T(8,128)(2,1)} %param.8, bf16[2,8,128,8,64]{4,3,1,2,0:T(8,128)(2,1)} %reshape.149), kind=kOutput, calls=%fused_computation | convolution fusion | flops 536870912 | bytes 23068672 | tf_op jit(solution)/shard_map/csaum,amx->csaux/dot_general | solution.py:91
  468.6 6.1 %copy.425 = f32[2,8,128,8,256]{4,3,2,1,0:T(8,128)} copy(f32[2,8,128,8,256]{4,3,1,0,2:T(8,128)S(1)} %convolution_bitcast_fusion) | data formatting | bytes 33554432 | tf_op jit(solution)/shard_map/csaum,amx->csaux/transpose | solution.py:91
  474.7 24.3 %reshape.150 = f32[2,8,4096,64]{3,2,1,0:T(8,128)} reshape(f32[2,8,128,8,256]{4,3,2,1,0:T(8,128)} %copy.425) | data formatting | bytes 33554432 | tf_op jit(solution)/shard_map/reshape | solution.py:94
  499.0 32.2 %fusion.18 = f32[2,8,512,64]{2,3,1,0:T(8,128)S(1)} fusion(f32[2,8,4096,64]{3,2,1,0:T(8,128)} %reshape.150, s32[4096]{0:T(1024)S(1)} %copy-done.14), kind=kOutput, calls=%fused_computation.48 | convolution fusion | flops 25771900928 | bytes 18890752 | tf_op jit(solution)/shard_map/rk,csrx->cskx/dot_general | solution.py:96
  531.2 2.8 copy.427
  534.0 4.0 reshape.151
  538.1 6.9 %copy.428 = f32[2,256,4,512]{3,2,1,0:T(4,128)} copy(f32[2,256,4,512]{3,1,0,2:T(8,128)} %get-tuple-element.13) | data formatting | bytes 8388608
  545.0 19.8 %reduce-scatter.2.cloned.1.call-done = f32[2,8,8192]{2,1,0:T(8,128)} async-done(((f32[2,8,32768]{2,1,0:T(8,128)}), f32[2,8,8192]{2,1,0:T(8,128)}) %reduce-scatter.2.cloned.1.call-update) | async-done | bytes 524304 | tf_op jit(solution)/shard_map/reduce_scatter | solution.py:146
  564.8 1.9 multiply_add_fusion
  (125 shorter events, 90.6 us)
Async XLA Ops:
  7.2 0.8 copy-start
  7.2 26.8 %all-gather.2.cloned.1.call-start = ((), (), s32[]{:S(2)}) async-start(), calls=%async_computation.3 | async-start | bytes 1310720 | tf_op jit(solution)/shard_map/all_gather | solution.py:106
  7.9 556.9 %reduce-scatter.2.cloned.1.call-start = ((), (), s32[]{:S(2)}) async-start(), calls=%async_computation.4 | async-start | bytes 2621440 | tf_op jit(solution)/shard_map/reduce_scatter | solution.py:146
  8.6 35.9 %copy-start.13 = (s32[4096]{0:T(1024)}, s32[4096]{0:T(1024)S(1)}, u32[]{:S(2)}) copy-start(s32[4096]{0:T(1024)S(1)} %eq.10) | copy-start | bytes 49156
  139.1 2.0 copy-start.16
  139.1 33.2 %copy-start.15 = (s32[4,1]{0,1:T(1,128)S(1)}, s32[4,1]{0,1:T(1,128)}, u32[]{:S(2)}) copy-start(s32[4,1]{0,1:T(1,128)} %param.13) | copy-start | bytes 52
  139.1 36.6 %copy-start.12 = (bf16[2,256,256]{2,1,0:T(8,128)(2,1)S(1)}, bf16[2,256,256]{2,1,0:T(8,128)(2,1)}, u32[]{:S(2)}) copy-start(bf16[2,256,256]{2,1,0:T(8,128)(2,1)} %param.10) | copy-start | bytes 786436
  139.3 36.5 %collective-permute-start = (bf16[2,256,4,512]{3,1,2,0:T(8,128)(2,1)S(1)}, bf16[2,256,4,512]{3,1,2,0:T(8,128)(2,1)}, u32[]{:S(2)}, u32[]{:S(2)}) collective-permute-start(bf16[2,256,4,512]{3,1,2,0:T(8,128)(2,1)S(1)} %bitcast.474), channel_id=1, source_target_pairs={{1,0},{2,1},{3,2},{0,3},{5,4},{6,5},{7,6},{4,7},{9,8},{10,9},{11,1... | collective-permute-start | bytes 6291464 | tf_op jit(solution)/shard_map/ppermute | solution.py:14
  272.9 1.0 copy-start.5
  272.9 1.8 copy-start.6
  292.6 2.5 copy-start.3
  292.6 2.5 copy-start.4
  313.8 2.4 copy-start.2
  349.0 6.0 %copy-start.8 = (f32[2,256,1,256]{3,1,0,2:T(8,128)S(1)}, f32[2,256,1,256]{3,1,0,2:T(8,128)}, u32[]{:S(2)}) copy-start(f32[2,256,1,256]{3,1,0,2:T(8,128)} %fusion.119) | copy-start | bytes 1572868
  352.8 6.1 %copy-start.9 = (f32[2,256,1,256]{3,1,0,2:T(8,128)S(1)}, f32[2,256,1,256]{3,1,0,2:T(8,128)}, u32[]{:S(2)}) copy-start(f32[2,256,1,256]{3,1,0,2:T(8,128)} %fusion.116) | copy-start | bytes 1572868
  355.0 11.7 %copy-start.7 = (f32[2,256,1024]{2,1,0:T(8,128)S(1)}, f32[2,256,1024]{2,1,0:T(8,128)}, u32[]{:S(2)}) copy-start(f32[2,256,1024]{2,1,0:T(8,128)} %dynamic_update_slice.66) | copy-start | bytes 6291460
  359.0 7.8 %copy-start.10 = (f32[2,256,1,256]{3,1,0,2:T(8,128)S(1)}, f32[2,256,1,256]{3,1,0,2:T(8,128)}, u32[]{:S(2)}) copy-start(f32[2,256,1,256]{3,1,0,2:T(8,128)} %fusion.110) | copy-start | bytes 1572868
  375.3 45.8 %collective-permute-start.1 = (f32[2,256,4,512]{3,1,0,2:T(8,128)S(1)}, f32[2,256,4,512]{3,1,0,2:T(8,128)S(1)}, u32[]{:S(2)}, u32[]{:S(2)}) collective-permute-start(f32[2,256,4,512]{3,1,0,2:T(8,128)S(1)} %slice.329), channel_id=1, source_target_pairs={{3,0},{0,1},{1,2},{2,3},{7,4},{4,5},{5,6},{6,7},{11,8},{8,9},{9,10... | collective-permute-start | bytes 12582920 | tf_op jit(solution)/shard_map/ppermute | solution.py:14
  474.7 24.3 %copy-start.14 = (s32[4096]{0:T(1024)S(1)}, s32[4096]{0:T(1024)}, u32[]{:S(2)}) copy-start(s32[4096]{0:T(1024)} %copy-done.13) | copy-start | bytes 49156
  538.1 26.7 %copy-start.11 = (bf16[2,8,8192]{2,1,0:T(8,128)(2,1)S(1)}, bf16[2,8,8192]{2,1,0:T(8,128)(2,1)}, u32[]{:S(2)}) copy-start(bf16[2,8,8192]{2,1,0:T(8,128)(2,1)} %param.7) | copy-start | bytes 786436
  538.1 28.6 %copy-start.1 = (s32[128,32,4]{0,2,1:T(4,128)S(1)}, s32[128,32,4]{0,2,1:T(4,128)}, u32[]{:S(2)}) copy-start(s32[128,32,4]{0,2,1:T(4,128)} %param.9) | copy-start | bytes 196612
Sparse Core Ops, SparseCore 0:
  9.7 24.2 all-gather.1
  538.2 26.5 reduce-scatter.1
where the time goes:
time: 585 us; the launch traced here: 574 us
  local copies, waits for them, and re-layouts  177 us (30%)
  matrix products  145 us (25%)
  waiting for transfers between devices  91.4 us (16%)
  blocking collectives  70.9 us (12%)
  between operations  44.8 us (8%)
  other arithmetic  42.4 us (7%)
    dynamic_update_slice x16, local copies, waits for them, and re-layouts, on_device(): lax.dynamic_update_slice_in_dim(summed, current + patch_grads[slot], star...  62.8 us
    dot_general x32, matrix products, right_mul(): jnp.einsum('qzy,yu->qzu', field, table, preferred_element_type=jnp.float32)  47.9 us
    ppermute x2, waiting for transfers between devices, from_behind(): return lax.ppermute(block, axis, route)  45.5 us
    dot_general x32, matrix products, left_mul(): jnp.einsum('zy,qyu->qzu', table, field, preferred_element_type=jnp.float32)  42.9 us
    all_to_all x1, blocking collectives, on_device(): lax.all_to_all(sinogram, 'ang', split_axis=2, concat_axis=1, tiled=True)  38.9 us
    dot_general x1, matrix products, back_project(): jnp.einsum('rk,csrx->cskx', choose, contrib, precision=lax.Precision.HIGH...  32.2 us
    all_to_all x1, blocking collectives, on_device(): lax.all_to_all(grad_rounded, 'ang', split_axis=1, concat_axis=2, tiled=True)  31.9 us
    all_gather x1, waiting for transfers between devices, on_device(): whole_volume = lax.all_gather(volume, 'pos', axis=2, tiled=True)  25.4 us
  transfers between devices with their start and end apart: 4, of which 3 were waited for; matrix products, arithmetic and copies ran while one was open for 2% of the time, Pallas kernels for 0%

commit v1 on v0

v1 whole, which is shorter than its diff:
```python
import functools
import math

import jax
import jax.numpy as jnp
from jax import lax
from jax.experimental import pallas as pl
from jax.experimental.pallas import tpu as pltpu
from jax.sharding import PartitionSpec as P

step_size = 0.1
f32 = jnp.float32
bf16 = jnp.bfloat16


def from_behind(block, axis, distance):
    devices = range(lax.axis_size(axis))
    route = [((i - distance) % len(devices), i) for i in devices]
    return lax.ppermute(block, axis, route)


def dft_tables(width):
    index = jnp.arange(width, dtype=jnp.int32)
    phase = index[:, None] * index[None, :] % width
    turn = 2.0 * math.pi / width * phase.astype(f32)
    cosine = (jnp.cos(turn) / math.sqrt(width)).astype(bf16)
    sine_neg = (-jnp.sin(turn) / math.sqrt(width)).astype(bf16)
    return (cosine, sine_neg)


def low_half(shape):
    return lax.broadcasted_iota(jnp.int32, shape, len(shape) - 1) < 64


def project_kernel(ids, vol, tiles, out, spread, *, feeds, pairs, angles):
    step = pl.program_id(0)
    owners, rows, width = vol.shape
    lo32 = low_half((rows, 128))

    @pl.when(step == 0)
    def _():
        per_owner = width // 128

        def expand(p, carry):
            at = pl.multiple_of(p * 128, 128)
            for o in range(owners):
                tile = vol[o, :, pl.ds(at, 128)].astype(f32)
                turned = pltpu.roll(tile, 64, 1)
                base = 2 * (o * per_owner + p)
                spread[base] = jnp.where(lo32, tile, turned).astype(bf16)
                spread[base + 1] = jnp.where(lo32, turned, tile).astype(bf16)
            return carry

        lax.fori_loop(0, per_owner, expand, 0, unroll=2)

    lo = low_half((rows, 128))
    for a in range(angles):
        at = (step * angles + a) * (2 * pairs * feeds)
        halves = []
        for parity in range(2):
            for bp in range(pairs):
                first = at + (2 * bp + parity) * feeds
                tile = [spread[ids[first + j]] for j in range(feeds)]
                halves.append(
                    jnp.concatenate(
                        [jnp.where(lo, tile[j], tile[j + 1]) for j in range(0, feeds, 2)], axis=1
                    )
                )
        picked = jnp.concatenate(halves, axis=0)
        twice = jnp.concatenate([tiles[a], tiles[a]], axis=0)
        both = lax.dot_general(
            picked, twice, (((1,), (1,)), ((), ())), preferred_element_type=f32
        )
        half = pairs * rows
        joined = jnp.where(low_half((half, 128)), both[:half], both[half:]).astype(bf16)
        for bp in range(pairs):
            out[0, a, :, bp * 128 : (bp + 1) * 128] = joined[bp * rows : (bp + 1) * rows]


def project(ids, vol, tiles, groups):
    owners, rows, width = vol.shape
    angle_count, block, span = tiles.shape
    feeds = span // block
    per_angle = ids.shape[0] // angle_count
    dets = per_angle // feeds
    angles = angle_count // groups
    blocks = owners * width // block
    return pl.pallas_call(
        functools.partial(project_kernel, feeds=feeds, pairs=dets // 2, angles=angles),
        name="project",
        out_shape=jax.ShapeDtypeStruct((groups, angles, rows, dets * block), bf16),
        grid_spec=pltpu.PrefetchScalarGridSpec(
            num_scalar_prefetch=1,
            grid=(groups,),
            in_specs=[
                pl.BlockSpec((owners, rows, width), lambda g, ids: (0, 0, 0)),
                pl.BlockSpec((angles, block, span), lambda g, ids: (g, 0, 0)),
            ],
            out_specs=pl.BlockSpec((1, angles, rows, dets * block), lambda g, ids: (g, 0, 0, 0)),
            scratch_shapes=[pltpu.VMEM((blocks, rows, 128), bf16)],
        ),
    )(ids, vol, tiles)


def exit_kernel(starts, counts, own, nextdoor, probe, amp, fwd, inv, grad, spill, ext, acc, *, slots):
    angle = pl.program_id(0)
    groups, _, rows, tile_width = own.shape
    side = probe.shape[1]
    n = groups * rows
    ext[:, :tile_width] = own[:, 0].reshape(n, tile_width)
    ext[:, tile_width:] = nextdoor[:, 0].reshape(n, side)
    acc[...] = jnp.zeros_like(acc)
    window = side + 128
    probe_re = probe[0].astype(f32)
    probe_im = probe[1].astype(f32)
    for slot in range(slots):
        start = starts[angle, slot]
        base = pl.multiple_of(start // 128 * 128, 128)
        shift = start - base
        source = lax.broadcasted_iota(jnp.int32, (window, side), 0)
        target = lax.broadcasted_iota(jnp.int32, (window, side), 1)
        pick = jnp.where(source - target == shift, 1.0, 0.0).astype(bf16)
        patch = jnp.dot(ext[:, pl.ds(base, window)], pick, preferred_element_type=f32)
        patch = patch.reshape(groups, 2, rows // 2, side)
        patch_re = patch[:, 0].reshape(side, side)
        patch_im = patch[:, 1].reshape(side, side)
        wave_re = (probe_re * patch_re - probe_im * patch_im).astype(bf16)
        wave_im = (probe_re * patch_im + probe_im * patch_re).astype(bf16)
        wave = jnp.concatenate([wave_re, wave_im], axis=0)
        half = jnp.dot(fwd[...], wave, preferred_element_type=f32).astype(bf16)
        half = jnp.concatenate([half[:side], half[side:]], axis=1)
        far = jnp.dot(half, inv[...], preferred_element_type=f32)
        far_re = far[:, :side]
        far_im = far[:, side:]
        power = far_re * far_re + far_im * far_im
        factor = amp[0, slot].astype(f32) * lax.rsqrt(jnp.maximum(power, 1.0)) - 1.0
        delta = jnp.concatenate(
            [(far_re * factor).astype(bf16), (far_im * factor).astype(bf16)], axis=0
        )
        back = jnp.dot(inv[...], delta, preferred_element_type=f32).astype(bf16)
        back = jnp.concatenate([back[:side], back[side:]], axis=1)
        near = jnp.dot(back, fwd[...], preferred_element_type=f32)
        near_re = near[:, :side]
        near_im = near[:, side:]
        live = jnp.where(slot < counts[angle, 0], 1.0, 0.0).astype(f32)
        grad_re = (probe_re * near_re + probe_im * near_im) * live
        grad_im = (probe_re * near_im - probe_im * near_re) * live
        both = jnp.concatenate(
            [
                grad_re.reshape(groups, 1, rows // 2, side),
                grad_im.reshape(groups, 1, rows // 2, side),
            ],
            axis=1,
        ).reshape(n, side)
        source = lax.broadcasted_iota(jnp.int32, (side, window), 1)
        target = lax.broadcasted_iota(jnp.int32, (side, window), 0)
        place = jnp.where(source - target == shift, 1.0, 0.0).astype(bf16)
        acc[:, pl.ds(base, window)] += jnp.dot(
            both.astype(bf16), place, preferred_element_type=f32
        )
    grad[:, 0] = acc[:, :tile_width].reshape(groups, rows, tile_width)
    spill[:, 0] = acc[:, tile_width:].astype(bf16).reshape(groups, rows, side)


def exit_gradient(starts, counts, own, nextdoor, probe, amp, fwd, inv):
    groups, angles, rows, tile_width = own.shape
    side = probe.shape[1]
    slots = starts.shape[1]
    n = groups * rows
    smem = pl.BlockSpec(memory_space=pltpu.SMEM)
    return pl.pallas_call(
        functools.partial(exit_kernel, slots=slots),
        name="exit_gradient",
        grid=(angles,),
        in_specs=[
            smem,
            smem,
            pl.BlockSpec((groups, 1, rows, tile_width), lambda a: (0, a, 0, 0)),
            pl.BlockSpec((groups, 1, rows, side), lambda a: (0, a, 0, 0)),
            pl.BlockSpec((2, side, side), lambda a: (0, 0, 0)),
            pl.BlockSpec((1, slots, side, side), lambda a: (a, 0, 0, 0)),
            pl.BlockSpec((2 * side, 2 * side), lambda a: (0, 0)),
            pl.BlockSpec((2 * side, 2 * side), lambda a: (0, 0)),
        ],
        out_specs=[
            pl.BlockSpec((groups, 1, rows, tile_width), lambda a: (0, a, 0, 0)),
            pl.BlockSpec((groups, 1, rows, side), lambda a: (0, a, 0, 0)),
        ],
        out_shape=[
            jax.ShapeDtypeStruct((groups, angles, rows, tile_width), f32),
            jax.ShapeDtypeStruct((groups, angles, rows, side), bf16),
        ],
        scratch_shapes=[
            pltpu.VMEM((n, tile_width + side), bf16),
            pltpu.VMEM((n, tile_width + side), f32),
        ],
    )(starts, counts, own, nextdoor, probe, amp, fwd, inv)


def back_kernel(ids, grad, tiles, out, *accs, feeds, pairs, angles):
    step = pl.program_id(0)
    owners, rows, width = out.shape
    blocks = accs[0].shape[0]

    @pl.when(step == 0)
    def _():
        def clear(i, carry):
            for acc in accs:
                acc[pl.ds(i * 8, 8)] = jnp.zeros((8, rows, 128), f32)
            return carry

        lax.fori_loop(0, blocks // 8, clear, 0)

    half = pairs * rows
    lo = low_half((half, 128))
    for a in range(angles):
        at = (step * angles + a) * (2 * pairs * feeds)
        flat = jnp.concatenate(
            [grad[0, a, :, bp * 128 : (bp + 1) * 128] for bp in range(pairs)], axis=0
        )
        zero = jnp.zeros_like(flat)
        halves = jnp.concatenate([jnp.where(lo, flat, zero), jnp.where(lo, zero, flat)], axis=0)
        twice = jnp.concatenate([tiles[a], tiles[a]], axis=0)
        contrib = jnp.dot(halves, twice, preferred_element_type=f32)
        for parity in range(2):
            for bp in range(pairs):
                first = at + (2 * bp + parity) * feeds
                top = (parity * pairs + bp) * rows
                where = [ids[first + j] for j in range(feeds)]
                old = [accs[j][where[j]] for j in range(feeds)]
                for j in range(feeds):
                    lane = j // 2 * 128
                    accs[j][where[j]] = old[j] + contrib[top : top + rows, lane : lane + 128]

    @pl.when(step == pl.num_programs(0) - 1)
    def _():
        lo = low_half((rows, 128))
        per_owner = width // 128

        def join(p, carry):
            at = pl.multiple_of(p * 128, 128)
            for o in range(owners):
                kb = 2 * (o * per_owner + p)
                even_lo = sum(accs[j][kb] for j in range(0, feeds, 2))
                even_hi = sum(accs[j][kb] for j in range(1, feeds, 2))
                odd_lo = sum(accs[j][kb + 1] for j in range(0, feeds, 2))
                odd_hi = sum(accs[j][kb + 1] for j in range(1, feeds, 2))
                out[o, :, pl.ds(at, 128)] = jnp.where(lo, even_lo, odd_hi) + pltpu.roll(
                    jnp.where(lo, odd_lo, even_hi), 64, 1
                )
            return carry

        lax.fori_loop(0, per_owner, join, 0, unroll=2)


def back_project(ids, grad, tiles, owners, coefs):
    groups, angles, rows, tile_width = grad.shape
    angle_count, block, span = tiles.shape
    feeds = span // block
    dets = tile_width // block
    blocks = coefs // block
    width = coefs // owners
    return pl.pallas_call(
        functools.partial(back_kernel, feeds=feeds, pairs=dets // 2, angles=angles),
        name="back_project",
        out_shape=jax.ShapeDtypeStruct((owners, rows, width), f32),
        grid_spec=pltpu.PrefetchScalarGridSpec(
            num_scalar_prefetch=1,
            grid=(groups,),
            in_specs=[
                pl.BlockSpec((1, angles, rows, tile_width), lambda g, ids: (g, 0, 0, 0)),
                pl.BlockSpec((angles, block, span), lambda g, ids: (g, 0, 0)),
            ],
            out_specs=pl.BlockSpec((owners, rows, width), lambda g, ids: (0, 0, 0)),
            scratch_shapes=[pltpu.VMEM((blocks, rows, 128), f32) for _ in range(feeds)],
        ),
    )(ids, grad, tiles)


def on_device(volume, radon_tiles, tile_blocks, probe_field, amplitudes, offsets, counts):
    n_pos = lax.axis_size("pos")
    n_ang = lax.axis_size("ang")
    pos_index = lax.axis_index("pos")
    parts, slab, width = volume.shape
    block = radon_tiles.shape[1]
    own_blocks = tile_blocks.shape[1] // n_pos
    tile_width = own_blocks * block
    side = probe_field.shape[1]
    angles = amplitudes.shape[0]
    rows = parts * slab

    whole = lax.all_gather(volume.reshape(rows, width), "pos", axis=0, tiled=False)
    ids = lax.dynamic_slice_in_dim(tile_blocks, pos_index * own_blocks, own_blocks, 1).reshape(-1)
    cosine, sine_neg = dft_tables(side)
    fwd = jnp.concatenate(
        [jnp.concatenate([cosine, -sine_neg], 1), jnp.concatenate([sine_neg, cosine], 1)], 0
    )
    inv = jnp.concatenate(
        [jnp.concatenate([cosine, sine_neg], 1), jnp.concatenate([-sine_neg, cosine], 1)], 0
    )
    starts = offsets - pos_index * tile_width

    sinogram = project(ids, whole, radon_tiles, n_ang)
    own = lax.all_to_all(sinogram, "ang", split_axis=0, concat_axis=0, tiled=True)
    nextdoor = from_behind(own[..., :side], "pos", -1)
    grad, spill = exit_gradient(
        starts, counts, own, nextdoor, probe_field, amplitudes, fwd, inv
    )
    spill = from_behind(spill, "pos", 1)
    grad = grad + jnp.pad(spill.astype(f32), ((0, 0), (0, 0), (0, 0), (0, tile_width - side)))
    back = lax.all_to_all(grad.astype(bf16), "ang", split_axis=0, concat_axis=0, tiled=True)
    partial = back_project(ids, back, radon_tiles, n_pos, n_pos * width)
    total = lax.psum_scatter(partial, "pos", scatter_dimension=0, tiled=False)
    new_volume = volume.astype(f32) + step_size * total.reshape(volume.shape)
    proj_grad = (
        grad.reshape(n_ang, angles, parts, slab, tile_width)
        .transpose(2, 0, 3, 1, 4)
        .reshape(parts, n_ang * slab, angles, tile_width)
    )
    return (new_volume, proj_grad)


def solution(mesh):
    in_specs = (
        P(None, "ang", "pos"),
        P(),
        P(),
        P(),
        P("ang", "pos", None, None),
        P("ang", "pos"),
        P("ang", "pos"),
    )
    out_specs = (P(None, "ang", "pos"), P(None, None, "ang", "pos"))
    return jax.shard_map(
        on_device, mesh=mesh, in_specs=in_specs, out_specs=out_specs, check_vma=False
    )
```

time: 585 us -> 258 us (0.44); the launches traced: 574 us -> 256 us
  local copies, waits for them, and re-layouts: 177 us -> 10.2 us
  matrix products: 145 us -> 0 us
  Pallas kernels: 0 us -> 83.8 us
  other arithmetic: 42.4 us -> 10.8 us
  between operations: 44.8 us -> 14.1 us
  waiting for transfers between devices: 91.4 us -> 64.8 us
    dot_general x68 -> x0, matrix products: 145 us -> none  [the longest x32 47.9 us: right_mul(): jnp.einsum('qzy,yu->qzu', field, table, preferred_element_type=jnp.float32)]
    pallas_call x0 -> x3, Pallas kernels: none -> 83.8 us  [the longest x1 31.7 us: exit_gradient(): pl.pallas_call(functools.partial(exit_kernel, slots=slots), name='exit_gr...]
    dynamic_update_slice x16 -> x0, local copies, waits for them, and re-layouts: 62.8 us -> none  [on_device(): lax.dynamic_update_slice_in_dim(summed, current + patch_grads[slot], star...]
    reshape x5 -> x1, local copies, waits for them, and re-layouts: 57.8 us -> 0.87 us  [on_device(): lax.dynamic_slice_in_dim(tile_blocks, pos_index * own_blocks, own_blocks, 1)]
    convert_element_type x4 -> x0, local copies, waits for them, and re-layouts: 26.2 us -> none  [the longest x1 15.5 us: project(): jnp.einsum('rk,cskx->csrx', choose, blocks, preferred_element_type=jnp.fl...]
    ppermute x2, waiting for transfers between devices: 45.5 us -> 20.3 us  [from_behind(): return lax.ppermute(block, axis, route)]
    add x9 -> x1, other arithmetic: 18.2 us -> 1.89 us  [on_device(): new_volume = volume.astype(f32) + step_size * total.reshape(volume.shape)]
    another operation x10 -> x0, other arithmetic: 14.3 us -> none  [the longest x5 12.7 us: on_device(): spread = jnp.stack(per_angle, axis=2)]
  transfers between devices with their start and end apart: 4 -> 4, of which waited for: 3 -> 4; matrix products, arithmetic and copies ran while one was open for 2% -> 5% of each run, Pallas kernels for 0% -> 0%
where the time goes in v1:
time: 258 us; the launch traced here: 256 us
  Pallas kernels  83.8 us (32%)
  blocking collectives  71 us (28%)
  waiting for transfers between devices  64.8 us (25%)
  between operations  14.1 us (5%)
  other arithmetic  10.8 us (4%)
  local copies, waits for them, and re-layouts  10.2 us (4%)
    all_to_all x1, blocking collectives, on_device(): lax.all_to_all(sinogram, 'ang', split_axis=0, concat_axis=0, tiled=True)  38.9 us
    all_to_all x1, blocking collectives, on_device(): lax.all_to_all(grad.astype(bf16), 'ang', split_axis=0, concat_axis=0, til...  32 us
    pallas_call x1, Pallas kernels, exit_gradient(): pl.pallas_call(functools.partial(exit_kernel, slots=slots), name='exit_gr...  31.7 us
    pallas_call x1, Pallas kernels, back_project(): pl.pallas_call(functools.partial(back_kernel, feeds=feeds, pairs=dets //...  27.1 us
    pallas_call x1, Pallas kernels, project(): pl.pallas_call(functools.partial(project_kernel, feeds=feeds, pairs=dets...  25 us
    all_gather x1, waiting for transfers between devices, on_device(): lax.all_gather(volume.reshape(rows, width), 'pos', axis=0, tiled=False)  24.9 us
    ppermute x2, waiting for transfers between devices, from_behind(): return lax.ppermute(block, axis, route)  20.3 us
    reduce_scatter x1, waiting for transfers between devices, on_device(): total = lax.psum_scatter(partial, 'pos', scatter_dimension=0, tiled=False)  19 us
  transfers between devices with their start and end apart: 4, of which 4 were waited for; matrix products, arithmetic and copies ran while one was open for 5% of the time, Pallas kernels for 0%

profile of v1, /device:TPU:1, one launch (start us, length us, event | category | flops | bytes accessed | tf_op | source)
XLA Modules:
  0.0 256.4 jit_solution(13918483706631258025)
XLA Ops:
  7.2 0.0 copy-start
  7.2 0.0 all-gather.2.cloned.1.call-start
  7.2 0.7 all-gather.2.cloned.1.call-update
  7.9 0.0 reduce-scatter.2.cloned.1.call-start
  8.0 0.0 copy-done
  8.0 0.3 copy.14
  8.3 0.9 reshape.15.ids
  9.2 24.9 %all-gather.2.cloned.1.call-done.vol = bf16[4,16,8192]{2,1,0:T(8,128)(2,1)} async-done(((bf16[1,16,8192]{2,1,0:T(8,128)(2,1)}), bf16[4,16,8192]{2,1,0:T(8,128)(2,1)}) %all-gather.2.cloned.1.call-update) | async-done | bytes 1048592 | tf_op jit(solution)/shard_map/all_gather | solution.py:292
  34.0 25.0 %project.1 = bf16[32,4,16,512]{3,2,1,0:T(8,128)(2,1)} custom-call(s32[4096]{0:T(1024)} %reshape.15.ids, bf16[4,16,8192]{2,1,0:T(8,128)(2,1)} %all-gather.2.cloned.1.call-done.vol, bf16[128,64,256]{2,1,0:T(8,128)(2,1)} %tiles.3), custom_call_target="tpu_custom_call" | custom-call | tf_op jit(solution)/shard_map/project/pallas_call | solution.py:88
  59.0 38.9 %all_to_all.10.own = bf16[32,4,16,512]{3,2,1,0:T(8,128)(2,1)S(1)} all-to-all(bf16[32,4,16,512]{3,2,1,0:T(8,128)(2,1)} %project.1), channel_id=1, replica_groups=mesh['ang'=32,'pos'=4] {'ang'}, dimensions={0} | all-to-all | bytes 4194304 | tf_op jit(solution)/shard_map/all_to_all | solution.py:304
  98.0 0.0 copy-start.1
  98.0 0.0 copy-start.4
  98.0 0.0 copy-start.3
  98.0 0.1 slice.4
  98.1 1.8 collective-permute-start
  99.9 0.0 copy-done.4
  99.9 0.7 copy.15.counts
  100.5 1.0 fusion.10
  101.5 1.1 multiply_convert_fusion
  102.6 1.1 fusion.3
  103.7 0.0 copy-done.3
  103.7 0.6 broadcast_subtract_fusion.starts
  104.3 8.2 %collective-permute-done.nextdoor = bf16[32,4,16,256]{3,2,1,0:T(8,128)(2,1)} collective-permute-done((bf16[32,4,16,256]{3,2,1,0:T(8,128)(2,1)S(1)}, bf16[32,4,16,256]{3,2,1,0:T(8,128)(2,1)}, u32[]{:S(2)}, u32[]{:S(2)}) %collective-permute-start) | collective-permute-done | bytes 1048608 | tf_op jit(solution)/shard_map/ppermute | solution.py:19
  112.5 0.0 copy-done.1
  112.5 31.7 %exit_gradient.1 = (f32[32,4,16,512]{3,2,1,0:T(8,128)}, bf16[32,4,16,256]{3,2,1,0:T(8,128)(2,1)}) custom-call(s32[4,4]{1,0:T(4,128)} %broadcast_subtract_fusion.starts, s32[4,1]{1,0:T(4,128)} %copy.15.counts, bf16[32,4,16,512]{3,2,1,0:T(8,128)(2,1)} %copy-done.1, bf16[32,4,16,256]{3,2,1,0:T(8,128)(2,1)} %collective-permute-done.nextdoor, ...), custom_call_target="tpu_custom_call" | custom-call | tf_op jit(solution)/shard_map/exit_gradient/pallas_call | solution.py:171
  144.2 0.0 collective-permute-start.1
  144.2 12.1 %collective-permute-done.1 = bf16[32,4,16,256]{3,2,1,0:T(8,128)(2,1)S(1)} collective-permute-done((bf16[32,4,16,256]{3,2,1,0:T(8,128)(2,1)}, bf16[32,4,16,256]{3,2,1,0:T(8,128)(2,1)S(1)}, u32[]{:S(2)}, u32[]{:S(2)}) %collective-permute-start.1) | collective-permute-done | bytes 1048608 | tf_op jit(solution)/shard_map/ppermute | solution.py:19
  156.2 5.1 %fusion = (f32[2,32,8,4,512]{4,2,0,3,1:T(8,128)}, bf16[32,4,16,512]{3,2,1,0:T(8,128)(2,1)S(1)}) fusion(f32[32,4,16,512]{3,2,1,0:T(8,128)} %get-tuple-element.4, bf16[32,4,16,256]{3,2,1,0:T(8,128)(2,1)S(1)} %collective-permute-done.1), kind=kLoop, calls=%fused_computation.1 | loop fusion | flops 3145728 | bytes 11534336 | tf_op jit(solution)/shard_map/transpose | solution.py:317
  161.4 32.0 %all_to_all.11.grad = bf16[32,4,16,512]{3,2,1,0:T(8,128)(2,1)} all-to-all(bf16[32,4,16,512]{3,2,1,0:T(8,128)(2,1)S(1)} %get-tuple-element.7), channel_id=1, replica_groups=mesh['ang'=32,'pos'=4] {'ang'}, dimensions={0} | all-to-all | bytes 4194304 | tf_op jit(solution)/shard_map/all_to_all | solution.py:311
  193.4 27.1 %back_project.1 = f32[4,16,8192]{2,1,0:T(8,128)} custom-call(s32[4096]{0:T(1024)} %reshape.15.ids, bf16[32,4,16,512]{3,2,1,0:T(8,128)(2,1)} %all_to_all.11.grad, bf16[128,64,256]{2,1,0:T(8,128)(2,1)} %tiles.3), custom_call_target="tpu_custom_call" | custom-call | tf_op jit(solution)/shard_map/back_project/pallas_call | solution.py:263
  220.5 0.0 reduce-scatter.2.cloned.1.call-update
  220.5 0.0 copy-start.2
  220.5 8.2 %copy.16 = f32[2,32,8,4,512]{4,3,2,1,0:T(4,128)} copy(f32[2,32,8,4,512]{4,2,0,3,1:T(8,128)} %get-tuple-element.6) | data formatting | bytes 8388608 | tf_op jit(solution)/shard_map/transpose | solution.py:317
  228.7 19.0 %reduce-scatter.2.cloned.1.call-done = f32[1,16,8192]{2,1,0:T(8,128)} async-done(((f32[4,16,8192]{2,1,0:T(8,128)}), f32[1,16,8192]{2,1,0:T(8,128)}) %reduce-scatter.2.cloned.1.call-update) | async-done | bytes 524304 | tf_op jit(solution)/shard_map/reduce_scatter | solution.py:313
  247.7 0.0 copy-done.2
  247.7 1.9 bitcast_add_fusion
  (1 shorter events, 0.0 us)
Async XLA Ops:
  7.2 0.8 copy-start
  7.2 26.8 %all-gather.2.cloned.1.call-start = ((), (), s32[]{:S(2)}) async-start(), calls=%async_computation.3 | async-start | bytes 1310720 | tf_op jit(solution)/shard_map/all_gather | solution.py:292
  7.9 239.7 %reduce-scatter.2.cloned.1.call-start = ((), (), s32[]{:S(2)}) async-start(), calls=%async_computation.4 | async-start | bytes 2621440 | tf_op jit(solution)/shard_map/reduce_scatter | solution.py:313
  98.0 14.5 %copy-start.1 = (bf16[32,4,16,512]{3,2,1,0:T(8,128)(2,1)}, bf16[32,4,16,512]{3,2,1,0:T(8,128)(2,1)S(1)}, u32[]{:S(2)}) copy-start(bf16[32,4,16,512]{3,2,1,0:T(8,128)(2,1)S(1)} %all_to_all.10.own) | copy-start | bytes 6291460
  98.0 1.9 copy-start.4
  98.0 5.7 %copy-start.3 = (s32[4,4]{1,0:T(4,128)S(1)}, s32[4,4]{1,0:T(4,128)}, u32[]{:S(2)}) copy-start(s32[4,4]{1,0:T(4,128)} %param.12) | copy-start | bytes 196
  98.1 14.4 %collective-permute-start = (bf16[32,4,16,256]{3,2,1,0:T(8,128)(2,1)S(1)}, bf16[32,4,16,256]{3,2,1,0:T(8,128)(2,1)}, u32[]{:S(2)}, u32[]{:S(2)}) collective-permute-start(bf16[32,4,16,256]{3,2,1,0:T(8,128)(2,1)S(1)} %slice.4), channel_id=1, source_target_pairs={{1,0},{2,1},{3,2},{0,3},{5,4},{6,5},{7,6},{4,7},{9,8},{10,9},{11,1... | collective-permute-start | bytes 3145736 | tf_op jit(solution)/shard_map/ppermute | solution.py:19
  144.2 12.1 %collective-permute-start.1 = (bf16[32,4,16,256]{3,2,1,0:T(8,128)(2,1)}, bf16[32,4,16,256]{3,2,1,0:T(8,128)(2,1)S(1)}, u32[]{:S(2)}, u32[]{:S(2)}) collective-permute-start(bf16[32,4,16,256]{3,2,1,0:T(8,128)(2,1)} %get-tuple-element.5), channel_id=1, source_target_pairs={{3,0},{0,1},{1,2},{2,3},{7,4},{4,5},{5,6},{6,7},{11,8},{8,9},{9,10... | collective-permute-start | bytes 3145736 | tf_op jit(solution)/shard_map/ppermute | solution.py:19
  220.5 27.2 %copy-start.2 = (bf16[2,8,8192]{2,1,0:T(8,128)(2,1)S(1)}, bf16[2,8,8192]{2,1,0:T(8,128)(2,1)}, u32[]{:S(2)}) copy-start(bf16[2,8,8192]{2,1,0:T(8,128)(2,1)} %param.7) | copy-start | bytes 786436
Sparse Core Ops, SparseCore 0:
  9.7 24.2 all-gather.1
  220.6 26.9 reduce-scatter.1

commit v2 on v1

--- a/solution.py
+++ b/solution.py
@@ -11,6 +11,7 @@
 step_size = 0.1
 f32 = jnp.float32
 bf16 = jnp.bfloat16
+MESH = pl.DeviceIdType.MESH
 
 
 def from_behind(block, axis, distance):
@@ -32,73 +33,188 @@
     return lax.broadcasted_iota(jnp.int32, shape, len(shape) - 1) < 64
 
 
-def project_kernel(ids, vol, tiles, out, spread, *, feeds, pairs, angles):
-    step = pl.program_id(0)
-    owners, rows, width = vol.shape
+def pos_peers():
+    pos = lax.axis_index("pos")
+    partner = pos + 1 - 2 * lax.rem(pos, 2)
+    cross = lax.rem(pos + 2, 4)
+    return pos, partner, cross
+
+
+def ang_peer(step, forward):
+    me = lax.axis_index("ang")
+    offset = lax.rem(13 * (step + 1), 32)
+    way = 1 - 2 * lax.rem(lax.axis_index("pos"), 2)
+    way = way if forward else -way
+    z = lax.rem(lax.div(me, 8) + way * lax.div(offset, 8) + 4, 4)
+    y = lax.rem(lax.rem(lax.div(me, 2), 4) + way * lax.rem(lax.div(offset, 2), 4) + 4, 4)
+    x = lax.rem(lax.rem(me, 2) + lax.rem(offset, 2), 2)
+    return z * 8 + y * 2 + x
+
+
+def remote(src, dst, send_sem, recv_sem, device):
+    return pltpu.make_async_remote_copy(
+        src_ref=src,
+        dst_ref=dst,
+        send_sem=send_sem,
+        recv_sem=recv_sem,
+        device_id=device,
+        device_id_type=MESH,
+    )
+
+
+def project_kernel(
+    ids, vol, tiles_hbm, out, gathered, tiles, spread, ready, tile_sem, own_sem, pos_send, pos_recv,
+    ang_send, ang_recv, *, feeds, pairs, angles, groups
+):
+    rows, width = vol.shape
+    me = lax.axis_index("ang")
+    pos, partner, cross = pos_peers()
+    far = lax.rem(partner + 2, 4)
+    load = pltpu.make_async_copy(tiles_hbm, tiles, tile_sem)
+    load.start()
+
+    barrier = pltpu.get_barrier_semaphore()
+    pl.semaphore_signal(barrier, inc=1, device_id={"pos": partner}, device_id_type=MESH)
+    pl.semaphore_signal(barrier, inc=1, device_id={"pos": cross}, device_id_type=MESH)
+
+    def greet(step, carry):
+        pl.semaphore_signal(
+            barrier, inc=1, device_id={"ang": ang_peer(step, True)}, device_id_type=MESH
+        )
+        return carry
+
+    lax.fori_loop(0, groups - 1, greet, 0)
+    pl.semaphore_wait(barrier, groups + 1)
+
+    to_cross = remote(vol, gathered.at[1], pos_send.at[1], pos_recv.at[1], {"pos": cross})
+    to_partner = remote(vol, gathered.at[0], pos_send.at[0], pos_recv.at[0], {"pos": partner})
+    onward = remote(
+        gathered.at[1], gathered.at[2], pos_send.at[2], pos_recv.at[2], {"pos": partner}
+    )
+    to_cross.start()
+    to_partner.start()
+
     lo32 = low_half((rows, 128))
-
-    @pl.when(step == 0)
-    def _():
-        per_owner = width // 128
-
-        def expand(p, carry):
+    per_owner = width // 128
+
+    def expand(source, owner):
+        def body(p, carry):
             at = pl.multiple_of(p * 128, 128)
-            for o in range(owners):
-                tile = vol[o, :, pl.ds(at, 128)].astype(f32)
-                turned = pltpu.roll(tile, 64, 1)
-                base = 2 * (o * per_owner + p)
-                spread[base] = jnp.where(lo32, tile, turned).astype(bf16)
-                spread[base + 1] = jnp.where(lo32, turned, tile).astype(bf16)
+            tile = source[:, pl.ds(at, 128)].astype(f32)
+            turned = pltpu.roll(tile, 64, 1)
+            base = 2 * (owner * per_owner + p)
+            spread[base] = jnp.where(lo32, tile, turned).astype(bf16)
+            spread[base + 1] = jnp.where(lo32, turned, tile).astype(bf16)
             return carry
 
-        lax.fori_loop(0, per_owner, expand, 0, unroll=2)
+        lax.fori_loop(0, per_owner, body, 0, unroll=4)
+
+    expand(vol, pos)
+    to_partner.wait_recv()
+    expand(gathered.at[0], partner)
+    to_cross.wait_recv()
+    onward.start()
+    expand(gathered.at[1], cross)
+    load.wait()
+    onward.wait_recv()
+    expand(gathered.at[2], far)
+
+    def outgoing(step):
+        group = ang_peer(step, True)
+        return remote(
+            ready.at[group], out.at[me], ang_send.at[step], ang_recv.at[step], {"ang": group}
+        )
+
+    def incoming(step):
+        group = ang_peer(step, False)
+        return remote(
+            ready.at[group], out.at[group], ang_send.at[step], ang_recv.at[step], {"ang": group}
+        )
 
     lo = low_half((rows, 128))
-    for a in range(angles):
-        at = (step * angles + a) * (2 * pairs * feeds)
-        halves = []
-        for parity in range(2):
+    half = pairs * rows
+    lo_half = low_half((half, 128))
+
+    def group_step(step, carry):
+        @pl.when(step > 0)
+        def _():
+            outgoing(step - 1).start()
+
+        group = ang_peer(step, True)
+        for a in range(angles):
+            at = (group * angles + a) * (2 * pairs * feeds)
+            halves = []
+            for parity in range(2):
+                for bp in range(pairs):
+                    first = at + (2 * bp + parity) * feeds
+                    tile = [spread[ids[first + j]] for j in range(feeds)]
+                    halves.append(
+                        jnp.concatenate(
+                            [jnp.where(lo, tile[j], tile[j + 1]) for j in range(0, feeds, 2)],
+                            axis=1,
+                        )
+                    )
+            picked = jnp.concatenate(halves, axis=0)
+            radon = tiles[group * angles + a]
+            twice = jnp.concatenate([radon, radon], axis=0)
+            both = lax.dot_general(
+                picked, twice, (((1,), (1,)), ((), ())), preferred_element_type=f32
+            )
+            joined = jnp.where(lo_half, both[:half], both[half:]).astype(bf16)
             for bp in range(pairs):
-                first = at + (2 * bp + parity) * feeds
-                tile = [spread[ids[first + j]] for j in range(feeds)]
-                halves.append(
-                    jnp.concatenate(
-                        [jnp.where(lo, tile[j], tile[j + 1]) for j in range(0, feeds, 2)], axis=1
-                    )
-                )
-        picked = jnp.concatenate(halves, axis=0)
-        twice = jnp.concatenate([tiles[a], tiles[a]], axis=0)
-        both = lax.dot_general(
-            picked, twice, (((1,), (1,)), ((), ())), preferred_element_type=f32
-        )
-        half = pairs * rows
-        joined = jnp.where(low_half((half, 128)), both[:half], both[half:]).astype(bf16)
-        for bp in range(pairs):
-            out[0, a, :, bp * 128 : (bp + 1) * 128] = joined[bp * rows : (bp + 1) * rows]
-
-
-def project(ids, vol, tiles, groups):
-    owners, rows, width = vol.shape
+                ready[group, a, :, bp * 128 : (bp + 1) * 128] = joined[bp * rows : (bp + 1) * rows]
+        return carry
+
+    lax.fori_loop(0, groups, group_step, 0)
+    to_cross.wait_send()
+    to_partner.wait_send()
+    onward.wait_send()
+    mine = pltpu.make_async_copy(ready.at[me], out.at[me], own_sem)
+    mine.start()
+
+    def finish(step, carry):
+        outgoing(step).wait_send()
+        incoming(step).wait_recv()
+        return carry
+
+    lax.fori_loop(0, groups - 1, finish, 0)
+    mine.wait()
+
+
+def project(ids, vol, tiles, groups, owners):
+    rows, width = vol.shape
     angle_count, block, span = tiles.shape
     feeds = span // block
     per_angle = ids.shape[0] // angle_count
     dets = per_angle // feeds
     angles = angle_count // groups
     blocks = owners * width // block
+    dma = pltpu.SemaphoreType.DMA
     return pl.pallas_call(
-        functools.partial(project_kernel, feeds=feeds, pairs=dets // 2, angles=angles),
+        functools.partial(
+            project_kernel, feeds=feeds, pairs=dets // 2, angles=angles, groups=groups
+        ),
         name="project",
         out_shape=jax.ShapeDtypeStruct((groups, angles, rows, dets * block), bf16),
-        grid_spec=pltpu.PrefetchScalarGridSpec(
-            num_scalar_prefetch=1,
-            grid=(groups,),
-            in_specs=[
-                pl.BlockSpec((owners, rows, width), lambda g, ids: (0, 0, 0)),
-                pl.BlockSpec((angles, block, span), lambda g, ids: (g, 0, 0)),
-            ],
-            out_specs=pl.BlockSpec((1, angles, rows, dets * block), lambda g, ids: (g, 0, 0, 0)),
-            scratch_shapes=[pltpu.VMEM((blocks, rows, 128), bf16)],
-        ),
+        in_specs=[
+            pl.BlockSpec(memory_space=pltpu.SMEM),
+            pl.BlockSpec(memory_space=pltpu.VMEM),
+            pl.BlockSpec(memory_space=pl.ANY),
+        ],
+        out_specs=pl.BlockSpec(memory_space=pl.ANY),
+        scratch_shapes=[
+            pltpu.VMEM((owners - 1, rows, width), bf16),
+            pltpu.VMEM(tiles.shape, bf16),
+            pltpu.VMEM((blocks, rows, 128), bf16),
+            pltpu.VMEM((groups, angles, rows, dets * block), bf16),
+            dma,
+            dma,
+            dma((3,)),
+            dma((3,)),
+            dma((groups - 1,)),
+            dma((groups - 1,)),
+        ],
+        compiler_params=pltpu.CompilerParams(collective_id=0, has_side_effects=True),
     )(ids, vol, tiles)
 
 
@@ -245,9 +361,10 @@
                 even_hi = sum(accs[j][kb] for j in range(1, feeds, 2))
                 odd_lo = sum(accs[j][kb + 1] for j in range(0, feeds, 2))
                 odd_hi = sum(accs[j][kb + 1] for j in range(1, feeds, 2))
-                out[o, :, pl.ds(at, 128)] = jnp.where(lo, even_lo, odd_hi) + pltpu.roll(
+                joined = jnp.where(lo, even_lo, odd_hi) + pltpu.roll(
                     jnp.where(lo, odd_lo, even_hi), 64, 1
                 )
+                out[o, :, pl.ds(at, 128)] = joined.astype(bf16)
             return carry
 
         lax.fori_loop(0, per_owner, join, 0, unroll=2)
@@ -263,7 +380,7 @@
     return pl.pallas_call(
         functools.partial(back_kernel, feeds=feeds, pairs=dets // 2, angles=angles),
         name="back_project",
-        out_shape=jax.ShapeDtypeStruct((owners, rows, width), f32),
+        out_shape=jax.ShapeDtypeStruct((owners, rows, width), bf16),
         grid_spec=pltpu.PrefetchScalarGridSpec(
             num_scalar_prefetch=1,
             grid=(groups,),
@@ -277,6 +394,96 @@
     )(ids, grad, tiles)
 
 
+def reduce_kernel(share, vol, out, near, mixed, far, send, recv):
+    rows, width = vol.shape
+    pos, partner, cross = pos_peers()
+    beyond = lax.rem(partner + 2, 4)
+    barrier = pltpu.get_barrier_semaphore()
+    pl.semaphore_signal(barrier, inc=1, device_id={"pos": partner}, device_id_type=MESH)
+    pl.semaphore_signal(barrier, inc=1, device_id={"pos": cross}, device_id_type=MESH)
+    pl.semaphore_wait(barrier, 2)
+
+    pieces = 4
+    piece = width // pieces
+    chunk = 512
+
+    def columns(k):
+        return pl.ds(k * piece, piece)
+
+    def side(k):
+        return remote(
+            share.at[beyond, :, columns(k)], near.at[0, :, columns(k)], send.at[k], recv.at[k],
+            {"pos": partner},
+        )
+
+    def over(k):
+        return remote(
+            mixed.at[:, columns(k)], far.at[:, columns(k)], send.at[pieces + k],
+            recv.at[pieces + k], {"pos": cross},
+        )
+
+    home = remote(
+        share.at[partner], near.at[1], send.at[2 * pieces], recv.at[2 * pieces], {"pos": partner}
+    )
+    for k in range(pieces):
+        side(k).start()
+    home.start()
+
+    def mix(k):
+        def body(i, carry):
+            at = pl.ds(pl.multiple_of(k * piece + i * chunk, chunk), chunk)
+            both = share[cross, :, at].astype(f32) + near[0, :, at].astype(f32)
+            mixed[:, at] = both.astype(bf16)
+            return carry
+
+        lax.fori_loop(0, piece // chunk, body, 0)
+
+    def total(k):
+        def body(i, carry):
+            at = pl.ds(pl.multiple_of(k * piece + i * chunk, chunk), chunk)
+            both = share[pos, :, at].astype(f32) + near[1, :, at].astype(f32)
+            out[:, at] = vol[:, at].astype(f32) + step_size * (both + far[:, at].astype(f32))
+            return carry
+
+        lax.fori_loop(0, piece // chunk, body, 0)
+
+    for k in range(pieces):
+        side(k).wait_recv()
+        mix(k)
+        if k > 0:
+            over(k - 1).start()
+    home.wait_recv()
+    over(pieces - 1).start()
+    for k in range(pieces):
+        over(k).wait_recv()
+        total(k)
+    for k in range(pieces):
+        side(k).wait_send()
+        over(k).wait_send()
+    home.wait_send()
+
+
+def reduce_step(share, vol):
+    rows, width = vol.shape
+    vmem = pl.BlockSpec(memory_space=pltpu.VMEM)
+    dma = pltpu.SemaphoreType.DMA
+    return pl.pallas_call(
+        reduce_kernel,
+        name="reduce_step",
+        out_shape=jax.ShapeDtypeStruct((rows, width), f32),
+        in_specs=[vmem, vmem],
+        out_specs=vmem,
+        scratch_shapes=[
+            pltpu.VMEM((2, rows, width), bf16),
+            pltpu.VMEM((rows, width), bf16),
+            pltpu.VMEM((rows, width), bf16),
+            dma((9,)),
+            dma((9,)),
+        ],
+        compiler_params=pltpu.CompilerParams(collective_id=1, has_side_effects=True),
+    )(share, vol)
+
+
 def on_device(volume, radon_tiles, tile_blocks, probe_field, amplitudes, offsets, counts):
     n_pos = lax.axis_size("pos")
     n_ang = lax.axis_size("ang")
@@ -289,7 +496,7 @@
     angles = amplitudes.shape[0]
     rows = parts * slab
 
-    whole = lax.all_gather(volume.reshape(rows, width), "pos", axis=0, tiled=False)
+    held = volume.reshape(rows, width)
     ids = lax.dynamic_slice_in_dim(tile_blocks, pos_index * own_blocks, own_blocks, 1).reshape(-1)
     cosine, sine_neg = dft_tables(side)
     fwd = jnp.concatenate(
@@ -300,8 +507,7 @@
     )
     starts = offsets - pos_index * tile_width
 
-    sinogram = project(ids, whole, radon_tiles, n_ang)
-    own = lax.all_to_all(sinogram, "ang", split_axis=0, concat_axis=0, tiled=True)
+    own = project(ids, held, radon_tiles, n_ang, n_pos)
     nextdoor = from_behind(own[..., :side], "pos", -1)
     grad, spill = exit_gradient(
         starts, counts, own, nextdoor, probe_field, amplitudes, fwd, inv
@@ -309,9 +515,8 @@
     spill = from_behind(spill, "pos", 1)
     grad = grad + jnp.pad(spill.astype(f32), ((0, 0), (0, 0), (0, 0), (0, tile_width - side)))
     back = lax.all_to_all(grad.astype(bf16), "ang", split_axis=0, concat_axis=0, tiled=True)
-    partial = back_project(ids, back, radon_tiles, n_pos, n_pos * width)
-    total = lax.psum_scatter(partial, "pos", scatter_dimension=0, tiled=False)
-    new_volume = volume.astype(f32) + step_size * total.reshape(volume.shape)
+    share = back_project(ids, back, radon_tiles, n_pos, n_pos * width)
+    new_volume = reduce_step(share, held).reshape(volume.shape)
     proj_grad = (
         grad.reshape(n_ang, angles, parts, slab, tile_width)
         .transpose(2, 0, 3, 1, 4)

time: 258 us -> 198 us (0.77)
  blocking collectives: 71 us -> 0 us
  Pallas kernels: 83.8 us -> 121 us
  waiting for transfers between devices: 64.8 us -> 41.2 us
  between operations: 14.1 us -> 0.7 us
  local copies, waits for them, and re-layouts: 10.2 us -> 16.2 us
  starting transfers between devices: 1.83 us -> 7.71 us
    all_to_all x2 -> x0, blocking collectives: 71 us -> none  [the longest x1 38.9 us: on_device(): lax.all_to_all(sinogram, 'ang', split_axis=0, concat_axis=0, tiled=True)]
    all_gather x1 -> x0, waiting for transfers between devices: 24.9 us -> none  [on_device(): lax.all_gather(volume.reshape(rows, width), 'pos', axis=0, tiled=False)]
    pallas_call x1, Pallas kernels: 25 us -> 48.6 us  [project(): pl.pallas_call(functools.partial(project_kernel, feeds=feeds, pairs=dets...]
    all_to_all x0 -> x1, waiting for transfers between devices: none -> 20 us  [on_device(): lax.all_to_all(grad.astype(bf16), 'ang', split_axis=0, concat_axis=0, til...]
    reduce_scatter x1 -> x0, waiting for transfers between devices: 19 us -> none  [on_device(): total = lax.psum_scatter(partial, 'pos', scatter_dimension=0, tiled=False)]
    pallas_call x0 -> x1, Pallas kernels: none -> 14.2 us  [reduce_step(): pl.pallas_call(reduce_kernel, name='reduce_step', out_shape=jax.ShapeDtyp...]
    all_to_all x0 -> x1, starting transfers between devices: none -> 6.97 us  [on_device(): lax.all_to_all(grad.astype(bf16), 'ang', split_axis=0, concat_axis=0, til...]
    unnamed x11 -> x12, local copies, waits for them, and re-layouts: 0.73 us -> 5.64 us
  transfers between devices with their start and end apart: 4 -> 3, of which waited for: 4 -> 3; matrix products, arithmetic and copies ran while one was open for 5% -> 6% of each run, Pallas kernels for 0% -> 0%
where the time goes in v2:
time: 198 us; the launch traced here: 197 us
  Pallas kernels  121 us (61%)
  waiting for transfers between devices  41.2 us (21%)
  local copies, waits for them, and re-layouts  16.2 us (8%)
  other arithmetic  9.6 us (5%)
  starting transfers between devices  7.71 us (4%)
    pallas_call x1, Pallas kernels, project(): pl.pallas_call(functools.partial(project_kernel, feeds=feeds, pairs=dets...  48.6 us
    pallas_call x1, Pallas kernels, exit_gradient(): pl.pallas_call(functools.partial(exit_kernel, slots=slots), name='exit_gr...  31.7 us
    pallas_call x1, Pallas kernels, back_project(): pl.pallas_call(functools.partial(back_kernel, feeds=feeds, pairs=dets //...  26.7 us
    ppermute x2, waiting for transfers between devices, from_behind(): return lax.ppermute(block, axis, route)  21.2 us
    all_to_all x1, waiting for transfers between devices, on_device(): lax.all_to_all(grad.astype(bf16), 'ang', split_axis=0, concat_axis=0, til...  20 us
    pallas_call x1, Pallas kernels, reduce_step(): pl.pallas_call(reduce_kernel, name='reduce_step', out_shape=jax.ShapeDtyp...  14.2 us
    transpose x1, local copies, waits for them, and re-layouts, on_device(): proj_grad = grad.reshape(n_ang, angles, parts, slab, tile_width).transpos...  8.14 us
    all_to_all x1, starting transfers between devices, on_device(): lax.all_to_all(grad.astype(bf16), 'ang', split_axis=0, concat_axis=0, til...  6.97 us
  transfers between devices with their start and end apart: 3, of which 3 were waited for; matrix products, arithmetic and copies ran while one was open for 6% of the time, Pallas kernels for 0%

profile of v2, /device:TPU:1, one launch (start us, length us, event | category | flops | bytes accessed | tf_op | source)
XLA Modules:
  0.0 196.6 jit_solution(2483505805261548552)
XLA Ops:
  0.6 0.0 copy-start
  0.6 0.8 copy-done
  1.5 0.3 copy.11
  1.7 0.9 reshape.19.ids
  2.6 0.0 copy-start.4
  2.6 0.0 copy-start.3
  2.6 48.6 %project.1.own = bf16[32,4,16,512]{3,2,1,0:T(8,128)(2,1)} custom-call(s32[4096]{0:T(1024)} %reshape.19.ids, bf16[16,8192]{1,0:T(8,128)(2,1)} %bitcast.9, bf16[128,64,256]{2,1,0:T(8,128)(2,1)} %tiles.1), custom_call_target="tpu_custom_call" | custom-call | tf_op jit(solution)/shard_map/project/pallas_call | solution.py:193
  51.3 1.3 slice.3
  52.6 0.7 collective-permute-start
  53.3 0.0 copy-done.4
  53.3 0.6 copy.12.counts
  53.9 1.0 fusion.10
  54.9 1.1 multiply_convert_fusion
  56.0 1.0 fusion.3
  57.1 0.0 copy-done.3
  57.1 0.6 broadcast_subtract_fusion.starts
  57.7 9.2 %collective-permute-done.nextdoor = bf16[32,4,16,256]{3,2,1,0:T(8,128)(2,1)S(1)} collective-permute-done((bf16[32,4,16,256]{3,2,1,0:T(8,128)(2,1)S(1)}, bf16[32,4,16,256]{3,2,1,0:T(8,128)(2,1)S(1)}, u32[]{:S(2)}, u32[]{:S(2)}) %collective-permute-start) | collective-permute-done | bytes 1048608 | tf_op jit(solution)/shard_map/ppermute | solution.py:20
  66.9 0.0 copy-start.2
  66.9 1.0 copy-done.2
  67.8 31.7 %exit_gradient.1 = (f32[32,4,16,512]{3,2,1,0:T(8,128)}, bf16[32,4,16,256]{3,2,1,0:T(8,128)(2,1)}) custom-call(s32[4,4]{1,0:T(4,128)} %broadcast_subtract_fusion.starts, s32[4,1]{1,0:T(4,128)} %copy.12.counts, bf16[32,4,16,512]{3,2,1,0:T(8,128)(2,1)} %project.1.own, bf16[32,4,16,256]{3,2,1,0:T(8,128)(2,1)} %copy-done.2, bf16[2,256,256]{2,1,0:T(8,128)(2,1)} %probe.1, ...), custom_call_target="tpu_custom_call" | custom-call | tf_op jit(solution)/shard_map/exit_gradient/pallas_call | solution.py:287
  99.5 0.0 collective-permute-start.1
  99.5 12.1 %collective-permute-done.1 = bf16[32,4,16,256]{3,2,1,0:T(8,128)(2,1)S(1)} collective-permute-done((bf16[32,4,16,256]{3,2,1,0:T(8,128)(2,1)}, bf16[32,4,16,256]{3,2,1,0:T(8,128)(2,1)S(1)}, u32[]{:S(2)}, u32[]{:S(2)}) %collective-permute-start.1) | collective-permute-done | bytes 1048608 | tf_op jit(solution)/shard_map/ppermute | solution.py:20
  111.6 5.9 %fusion = (f32[2,32,8,4,512]{4,2,0,3,1:T(8,128)}, bf16[32,4,16,512]{3,2,1,0:T(8,128)(2,1)}) fusion(f32[32,4,16,512]{3,2,1,0:T(8,128)} %get-tuple-element.4, bf16[32,4,16,256]{3,2,1,0:T(8,128)(2,1)S(1)} %collective-permute-done.1), kind=kLoop, calls=%fused_computation.1 | loop fusion | flops 3145728 | bytes 11534336 | tf_op jit(solution)/shard_map/transpose | solution.py:522
  117.4 7.0 %all-to-all-start = ((bf16[32,4,16,512]{3,2,1,0:T(8,128)(2,1)}), bf16[32,4,16,512]{3,2,1,0:T(8,128)(2,1)S(1)}, u32[]{:S(2)}, u32[]{:S(2)}) async-start(bf16[32,4,16,512]{3,2,1,0:T(8,128)(2,1)} %get-tuple-element.7), calls=%async_computation | async-start | bytes 4194304 | tf_op jit(solution)/shard_map/all_to_all | solution.py:517
  124.4 8.1 %copy.13 = f32[2,32,8,4,512]{4,3,2,1,0:T(4,128)} copy(f32[2,32,8,4,512]{4,2,0,3,1:T(8,128)} %get-tuple-element.6) | data formatting | bytes 8388608 | tf_op jit(solution)/shard_map/transpose | solution.py:522
  132.6 20.0 %all-to-all-done.grad = bf16[32,4,16,512]{3,2,1,0:T(8,128)(2,1)S(1)} async-done(((bf16[32,4,16,512]{3,2,1,0:T(8,128)(2,1)}), bf16[32,4,16,512]{3,2,1,0:T(8,128)(2,1)S(1)}, u32[]{:S(2)}, u32[]{:S(2)}) %all-to-all-start) | async-done | bytes 2097184 | tf_op jit(solution)/shard_map/all_to_all | solution.py:517
  152.5 0.0 copy-start.1
  152.5 1.3 copy-done.1
  153.9 26.7 %back_project.1.share = bf16[4,16,8192]{2,1,0:T(8,128)(2,1)} custom-call(s32[4096]{0:T(1024)} %reshape.19.ids, bf16[32,4,16,512]{3,2,1,0:T(8,128)(2,1)} %copy-done.1, bf16[128,64,256]{2,1,0:T(8,128)(2,1)} %tiles.1), custom_call_target="tpu_custom_call" | custom-call | tf_op jit(solution)/shard_map/back_project/pallas_call | solution.py:380
  180.6 14.2 %reduce_step.1 = f32[16,8192]{1,0:T(8,128)} custom-call(bf16[4,16,8192]{2,1,0:T(8,128)(2,1)} %back_project.1.share, bf16[16,8192]{1,0:T(8,128)(2,1)} %bitcast.10), custom_call_target="tpu_custom_call" | custom-call | tf_op jit(solution)/shard_map/reduce_step/pallas_call | solution.py:470
  194.8 1.9 copy.15
  (1 shorter events, 0.0 us)
Async XLA Ops:
  0.6 0.8 copy-start
  2.6 50.7 %copy-start.4 = (s32[4,1]{0,1:T(1,128)S(1)}, s32[4,1]{0,1:T(1,128)}, u32[]{:S(2)}) copy-start(s32[4,1]{0,1:T(1,128)} %param.13) | copy-start | bytes 52
  2.6 54.5 %copy-start.3 = (s32[4,4]{1,0:T(4,128)S(1)}, s32[4,4]{1,0:T(4,128)}, u32[]{:S(2)}) copy-start(s32[4,4]{1,0:T(4,128)} %param.12) | copy-start | bytes 196
  52.6 14.3 %collective-permute-start = (bf16[32,4,16,256]{3,2,1,0:T(8,128)(2,1)S(1)}, bf16[32,4,16,256]{3,2,1,0:T(8,128)(2,1)S(1)}, u32[]{:S(2)}, u32[]{:S(2)}) collective-permute-start(bf16[32,4,16,256]{3,2,1,0:T(8,128)(2,1)S(1)} %slice.3), channel_id=1, source_target_pairs={{1,0},{2,1},{3,2},{0,3},{5,4},{6,5},{7,6},{4,7},{9,8},{10,9},{11,1... | collective-permute-start | bytes 3145736 | tf_op jit(solution)/shard_map/ppermute | solution.py:20
  66.9 1.0 copy-start.2
  99.5 12.1 %collective-permute-start.1 = (bf16[32,4,16,256]{3,2,1,0:T(8,128)(2,1)}, bf16[32,4,16,256]{3,2,1,0:T(8,128)(2,1)S(1)}, u32[]{:S(2)}, u32[]{:S(2)}) collective-permute-start(bf16[32,4,16,256]{3,2,1,0:T(8,128)(2,1)} %get-tuple-element.5), channel_id=1, source_target_pairs={{3,0},{0,1},{1,2},{2,3},{7,4},{4,5},{5,6},{6,7},{11,8},{8,9},{9,10... | collective-permute-start | bytes 3145736 | tf_op jit(solution)/shard_map/ppermute | solution.py:20
  117.4 35.1 %all-to-all-start = ((bf16[32,4,16,512]{3,2,1,0:T(8,128)(2,1)}), bf16[32,4,16,512]{3,2,1,0:T(8,128)(2,1)S(1)}, u32[]{:S(2)}, u32[]{:S(2)}) async-start(bf16[32,4,16,512]{3,2,1,0:T(8,128)(2,1)} %get-tuple-element.7), calls=%async_computation | async-start | bytes 4194304 | tf_op jit(solution)/shard_map/all_to_all | solution.py:517
  152.5 1.3 copy-start.1

commit v3 on v2

--- a/solution.py
+++ b/solution.py
@@ -12,12 +12,6 @@
 f32 = jnp.float32
 bf16 = jnp.bfloat16
 MESH = pl.DeviceIdType.MESH
-
-
-def from_behind(block, axis, distance):
-    devices = range(lax.axis_size(axis))
-    route = [((i - distance) % len(devices), i) for i in devices]
-    return lax.ppermute(block, axis, route)
 
 
 def dft_tables(width):
@@ -218,99 +212,226 @@
     )(ids, vol, tiles)
 
 
-def exit_kernel(starts, counts, own, nextdoor, probe, amp, fwd, inv, grad, spill, ext, acc, *, slots):
-    angle = pl.program_id(0)
-    groups, _, rows, tile_width = own.shape
+def exit_kernel(
+    starts, counts, own, probe, amp, fwd, inv, grad, back, landed, strip, summed, rounded, patches,
+    spill_out, spill_in, load_sem, store_sem, own_sem, pos_send, pos_recv, ang_send, ang_recv,
+    *, slots, groups, angles
+):
+    rows, tile_width = own.shape[2:]
     side = probe.shape[1]
     n = groups * rows
-    ext[:, :tile_width] = own[:, 0].reshape(n, tile_width)
-    ext[:, tile_width:] = nextdoor[:, 0].reshape(n, side)
-    acc[...] = jnp.zeros_like(acc)
+    me = lax.axis_index("ang")
+    pos = lax.axis_index("pos")
+    after = lax.rem(pos + 1, 4)
+    before = lax.rem(pos + 3, 4)
+
+    def load(a):
+        return pltpu.make_async_copy(
+            own.at[:, a], landed.at[a, :, :, :tile_width], load_sem.at[a]
+        )
+
+    def halo(a):
+        return remote(
+            own.at[:, a, :, :side], landed.at[a, :, :, tile_width:], pos_send.at[0, a],
+            pos_recv.at[0, a], {"pos": before},
+        )
+
+    def spill(a):
+        return remote(
+            spill_out.at[a], spill_in.at[a], pos_send.at[1, a], pos_recv.at[1, a], {"pos": after}
+        )
+
+    def outgoing(a, step):
+        group = ang_peer(step, True)
+        return remote(
+            rounded.at[a, group], back.at[me, a], ang_send.at[a, step], ang_recv.at[a, step],
+            {"ang": group},
+        )
+
+    def incoming(a, step):
+        group = ang_peer(step, False)
+        return remote(
+            rounded.at[a, group], back.at[group, a], ang_send.at[a, step], ang_recv.at[a, step],
+            {"ang": group},
+        )
+
+    def keep(a):
+        return pltpu.make_async_copy(rounded.at[a, me], back.at[me, a], own_sem.at[a])
+
+    def store(a, c):
+        half = rows // 2
+        return pltpu.make_async_copy(
+            summed.at[a, :, c * half : (c + 1) * half], grad.at[c, :, :, a, :], store_sem.at[a, c]
+        )
+
+    for a in range(angles):
+        load(a).start()
+    barrier = pltpu.get_barrier_semaphore()
+    pl.semaphore_signal(barrier, inc=1, device_id={"pos": before}, device_id_type=MESH)
+    pl.semaphore_signal(barrier, inc=1, device_id={"pos": after}, device_id_type=MESH)
+
+    def greet(step, carry):
+        pl.semaphore_signal(
+            barrier, inc=1, device_id={"ang": ang_peer(step, True)}, device_id_type=MESH
+        )
+        return carry
+
+    lax.fori_loop(0, groups - 1, greet, 0)
+    pl.semaphore_wait(barrier, groups + 1)
+    for a in range(angles):
+        halo(a).start()
+
     window = side + 128
     probe_re = probe[0].astype(f32)
     probe_im = probe[1].astype(f32)
-    for slot in range(slots):
-        start = starts[angle, slot]
-        base = pl.multiple_of(start // 128 * 128, 128)
-        shift = start - base
-        source = lax.broadcasted_iota(jnp.int32, (window, side), 0)
-        target = lax.broadcasted_iota(jnp.int32, (window, side), 1)
-        pick = jnp.where(source - target == shift, 1.0, 0.0).astype(bf16)
-        patch = jnp.dot(ext[:, pl.ds(base, window)], pick, preferred_element_type=f32)
-        patch = patch.reshape(groups, 2, rows // 2, side)
-        patch_re = patch[:, 0].reshape(side, side)
-        patch_im = patch[:, 1].reshape(side, side)
-        wave_re = (probe_re * patch_re - probe_im * patch_im).astype(bf16)
-        wave_im = (probe_re * patch_im + probe_im * patch_re).astype(bf16)
-        wave = jnp.concatenate([wave_re, wave_im], axis=0)
-        half = jnp.dot(fwd[...], wave, preferred_element_type=f32).astype(bf16)
-        half = jnp.concatenate([half[:side], half[side:]], axis=1)
-        far = jnp.dot(half, inv[...], preferred_element_type=f32)
-        far_re = far[:, :side]
-        far_im = far[:, side:]
-        power = far_re * far_re + far_im * far_im
-        factor = amp[0, slot].astype(f32) * lax.rsqrt(jnp.maximum(power, 1.0)) - 1.0
-        delta = jnp.concatenate(
-            [(far_re * factor).astype(bf16), (far_im * factor).astype(bf16)], axis=0
-        )
-        back = jnp.dot(inv[...], delta, preferred_element_type=f32).astype(bf16)
-        back = jnp.concatenate([back[:side], back[side:]], axis=1)
-        near = jnp.dot(back, fwd[...], preferred_element_type=f32)
-        near_re = near[:, :side]
-        near_im = near[:, side:]
-        live = jnp.where(slot < counts[angle, 0], 1.0, 0.0).astype(f32)
-        grad_re = (probe_re * near_re + probe_im * near_im) * live
-        grad_im = (probe_re * near_im - probe_im * near_re) * live
-        both = jnp.concatenate(
+
+    def compute(a):
+        load(a).wait()
+        halo(a).wait_recv()
+        for lane in range((tile_width + side) // 128):
+            part = landed[a, :, :, lane * 128 : (lane + 1) * 128]
+            strip[lane] = part.reshape(n, 128)
+        for slot in range(slots):
+            start = starts[a, slot]
+            block = lax.div(start, 128)
+            shift = start - block * 128
+            source = lax.broadcasted_iota(jnp.int32, (window, side), 0)
+            target = lax.broadcasted_iota(jnp.int32, (window, side), 1)
+            pick = jnp.where(source - target == shift, 1.0, 0.0).astype(bf16)
+            view = jnp.concatenate([strip[block + i] for i in range(window // 128)], axis=1)
+            patch = jnp.dot(view, pick, preferred_element_type=f32)
+            patch = patch.reshape(groups, 2, rows // 2, side)
+            patch_re = patch[:, 0].reshape(side, side)
+            patch_im = patch[:, 1].reshape(side, side)
+            wave_re = (probe_re * patch_re - probe_im * patch_im).astype(bf16)
+            wave_im = (probe_re * patch_im + probe_im * patch_re).astype(bf16)
+            wave = jnp.concatenate([wave_re, wave_im], axis=0)
+            half = jnp.dot(fwd[...], wave, preferred_element_type=f32).astype(bf16)
+            half = jnp.concatenate([half[:side], half[side:]], axis=1)
+            far = jnp.dot(half, inv[...], preferred_element_type=f32)
+            far_re = far[:, :side]
+            far_im = far[:, side:]
+            power = far_re * far_re + far_im * far_im
+            factor = amp[a, slot].astype(f32) * lax.rsqrt(jnp.maximum(power, 1.0)) - 1.0
+            delta = jnp.concatenate(
+                [(far_re * factor).astype(bf16), (far_im * factor).astype(bf16)], axis=0
+            )
+            turned = jnp.dot(inv[...], delta, preferred_element_type=f32).astype(bf16)
+            turned = jnp.concatenate([turned[:side], turned[side:]], axis=1)
+            near = jnp.dot(turned, fwd[...], preferred_element_type=f32)
+            near_re = near[:, :side]
+            near_im = near[:, side:]
+            live = jnp.minimum(jnp.maximum(counts[a, 0] - slot, 0), 1).astype(f32)
+            grad_re = (probe_re * near_re + probe_im * near_im) * live
+            grad_im = (probe_re * near_im - probe_im * near_re) * live
+            both = jnp.concatenate(
+                [
+                    grad_re.reshape(groups, 1, rows // 2, side),
+                    grad_im.reshape(groups, 1, rows // 2, side),
+                ],
+                axis=1,
+            ).reshape(n, side)
+            patches[:, slot * side : (slot + 1) * side] = both.astype(bf16)
+        whole = tile_width + side
+        source = lax.broadcasted_iota(jnp.int32, (side, whole), 1)
+        target = lax.broadcasted_iota(jnp.int32, (side, whole), 0)
+        place = jnp.concatenate(
             [
-                grad_re.reshape(groups, 1, rows // 2, side),
-                grad_im.reshape(groups, 1, rows // 2, side),
+                jnp.where(source - target == starts[a, slot], 1.0, 0.0).astype(bf16)
+                for slot in range(slots)
             ],
-            axis=1,
-        ).reshape(n, side)
-        source = lax.broadcasted_iota(jnp.int32, (side, window), 1)
-        target = lax.broadcasted_iota(jnp.int32, (side, window), 0)
-        place = jnp.where(source - target == shift, 1.0, 0.0).astype(bf16)
-        acc[:, pl.ds(base, window)] += jnp.dot(
-            both.astype(bf16), place, preferred_element_type=f32
-        )
-    grad[:, 0] = acc[:, :tile_width].reshape(groups, rows, tile_width)
-    spill[:, 0] = acc[:, tile_width:].astype(bf16).reshape(groups, rows, side)
-
-
-def exit_gradient(starts, counts, own, nextdoor, probe, amp, fwd, inv):
+            axis=0,
+        )
+        over = jnp.dot(patches[...], place[:, tile_width:], preferred_element_type=f32)
+        spill_out[a] = over.astype(bf16).reshape(groups, rows, side)
+        inside = jnp.dot(patches[...], place[:, :tile_width], preferred_element_type=f32)
+        summed[a] = inside.reshape(groups, rows, tile_width)
+        spill(a).start()
+
+    def send(a):
+        spill(a).wait_recv()
+
+        def body(g, carry):
+            left = summed[a, g, :, :side] + spill_in[a, g].astype(f32)
+            summed[a, g, :, :side] = left
+            rounded[a, g, :, :side] = left.astype(bf16)
+            rounded[a, g, :, side:] = summed[a, g, :, side:].astype(bf16)
+            return carry
+
+        lax.fori_loop(0, groups, body, 0, unroll=2)
+        for c in range(2):
+            store(a, c).start()
+
+        def depart(step, carry):
+            outgoing(a, step).start()
+            return carry
+
+        lax.fori_loop(0, groups - 1, depart, 0)
+        keep(a).start()
+
+    def angle_step(a, carry):
+        compute(a)
+
+        @pl.when(a > 0)
+        def _():
+            send(a - 1)
+
+        return carry
+
+    lax.fori_loop(0, angles, angle_step, 0)
+    send(angles - 1)
+    for a in range(angles):
+        halo(a).wait_send()
+        spill(a).wait_send()
+        keep(a).wait()
+        for c in range(2):
+            store(a, c).wait()
+
+    def finish(step, carry):
+        for a in range(angles):
+            outgoing(a, step).wait_send()
+            incoming(a, step).wait_recv()
+        return carry
+
+    lax.fori_loop(0, groups - 1, finish, 0)
+
+
+def exit_gradient(starts, counts, own, probe, amp, fwd, inv):
     groups, angles, rows, tile_width = own.shape
     side = probe.shape[1]
     slots = starts.shape[1]
     n = groups * rows
     smem = pl.BlockSpec(memory_space=pltpu.SMEM)
+    vmem = pl.BlockSpec(memory_space=pltpu.VMEM)
+    hbm = pl.BlockSpec(memory_space=pl.ANY)
+    dma = pltpu.SemaphoreType.DMA
     return pl.pallas_call(
-        functools.partial(exit_kernel, slots=slots),
+        functools.partial(exit_kernel, slots=slots, groups=groups, angles=angles),
         name="exit_gradient",
-        grid=(angles,),
-        in_specs=[
-            smem,
-            smem,
-            pl.BlockSpec((groups, 1, rows, tile_width), lambda a: (0, a, 0, 0)),
-            pl.BlockSpec((groups, 1, rows, side), lambda a: (0, a, 0, 0)),
-            pl.BlockSpec((2, side, side), lambda a: (0, 0, 0)),
-            pl.BlockSpec((1, slots, side, side), lambda a: (a, 0, 0, 0)),
-            pl.BlockSpec((2 * side, 2 * side), lambda a: (0, 0)),
-            pl.BlockSpec((2 * side, 2 * side), lambda a: (0, 0)),
-        ],
-        out_specs=[
-            pl.BlockSpec((groups, 1, rows, tile_width), lambda a: (0, a, 0, 0)),
-            pl.BlockSpec((groups, 1, rows, side), lambda a: (0, a, 0, 0)),
-        ],
+        in_specs=[smem, smem, hbm, vmem, vmem, vmem, vmem],
+        out_specs=[hbm, hbm],
         out_shape=[
-            jax.ShapeDtypeStruct((groups, angles, rows, tile_width), f32),
-            jax.ShapeDtypeStruct((groups, angles, rows, side), bf16),
+            jax.ShapeDtypeStruct((2, groups, rows // 2, angles, tile_width), f32),
+            jax.ShapeDtypeStruct((groups, angles, rows, tile_width), bf16),
         ],
         scratch_shapes=[
-            pltpu.VMEM((n, tile_width + side), bf16),
-            pltpu.VMEM((n, tile_width + side), f32),
+            pltpu.VMEM((angles, groups, rows, tile_width + side), bf16),
+            pltpu.VMEM(((tile_width + side) // 128, n, 128), bf16),
+            pltpu.VMEM((angles, groups, rows, tile_width), f32),
+            pltpu.VMEM((angles, groups, rows, tile_width), bf16),
+            pltpu.VMEM((n, slots * side), bf16),
+            pltpu.VMEM((angles, groups, rows, side), bf16),
+            pltpu.VMEM((angles, groups, rows, side), bf16),
+            dma((angles,)),
+            dma((angles, 2)),
+            dma((angles,)),
+            dma((2, angles)),
+            dma((2, angles)),
+            dma((angles, groups - 1)),
+            dma((angles, groups - 1)),
         ],
-    )(starts, counts, own, nextdoor, probe, amp, fwd, inv)
+        compiler_params=pltpu.CompilerParams(collective_id=2, has_side_effects=True),
+    )(starts, counts, own, probe, amp, fwd, inv)
 
 
 def back_kernel(ids, grad, tiles, out, *accs, feeds, pairs, angles):
@@ -508,20 +629,10 @@
     starts = offsets - pos_index * tile_width
 
     own = project(ids, held, radon_tiles, n_ang, n_pos)
-    nextdoor = from_behind(own[..., :side], "pos", -1)
-    grad, spill = exit_gradient(
-        starts, counts, own, nextdoor, probe_field, amplitudes, fwd, inv
-    )
-    spill = from_behind(spill, "pos", 1)
-    grad = grad + jnp.pad(spill.astype(f32), ((0, 0), (0, 0), (0, 0), (0, tile_width - side)))
-    back = lax.all_to_all(grad.astype(bf16), "ang", split_axis=0, concat_axis=0, tiled=True)
+    grad, back = exit_gradient(starts, counts, own, probe_field, amplitudes, fwd, inv)
     share = back_project(ids, back, radon_tiles, n_pos, n_pos * width)
     new_volume = reduce_step(share, held).reshape(volume.shape)
-    proj_grad = (
-        grad.reshape(n_ang, angles, parts, slab, tile_width)
-        .transpose(2, 0, 3, 1, 4)
-        .reshape(parts, n_ang * slab, angles, tile_width)
-    )
+    proj_grad = grad.reshape(parts, n_ang * slab, angles, tile_width)
     return (new_volume, proj_grad)
 
 

time: 198 us -> 165 us (0.83)
  waiting for transfers between devices: 41.2 us -> 0 us
  Pallas kernels: 121 us -> 150 us
  starting transfers between devices: 7.71 us -> 0 us
  local copies, waits for them, and re-layouts: 16.2 us -> 9.25 us
  other arithmetic: 9.6 us -> 4.45 us
    pallas_call x1, Pallas kernels: 31.7 us -> 62.2 us  [exit_gradient(): pl.pallas_call(functools.partial(exit_kernel, slots=slots, groups=groups,...]
    ppermute x2 -> x0, waiting for transfers between devices: 21.2 us -> none  [from_behind(): return lax.ppermute(block, axis, route)]
    all_to_all x1 -> x0, waiting for transfers between devices: 20 us -> none  [on_device(): lax.all_to_all(grad.astype(bf16), 'ang', split_axis=0, concat_axis=0, til...]
    transpose x1 -> x0, local copies, waits for them, and re-layouts: 8.14 us -> none  [on_device(): proj_grad = grad.reshape(n_ang, angles, parts, slab, tile_width).transpos...]
    all_to_all x1 -> x0, starting transfers between devices: 6.97 us -> none  [on_device(): lax.all_to_all(grad.astype(bf16), 'ang', split_axis=0, concat_axis=0, til...]
    transpose x1 -> x0, other arithmetic: 5.86 us -> none  [on_device(): proj_grad = grad.reshape(n_ang, angles, parts, slab, tile_width).transpos...]
    unnamed x12 -> x5, local copies, waits for them, and re-layouts: 5.64 us -> 8.13 us
    pallas_call x1, Pallas kernels: 14.2 us -> 12.2 us  [reduce_step(): pl.pallas_call(reduce_kernel, name='reduce_step', out_shape=jax.ShapeDtyp...]
  transfers between devices with their start and end apart: 3 -> 0, of which waited for: 3 -> 0; matrix products, arithmetic and copies ran while one was open for 6% -> 0% of each run, Pallas kernels for 0% -> 0%
where the time goes in v3:
time: 165 us; the launch traced here: 164 us
  Pallas kernels  150 us (91%)
  local copies, waits for them, and re-layouts  9.25 us (6%)
  other arithmetic  4.45 us (3%)
    pallas_call x1, Pallas kernels, exit_gradient(): pl.pallas_call(functools.partial(exit_kernel, slots=slots, groups=groups,...  62.2 us
    pallas_call x1, Pallas kernels, project(): pl.pallas_call(functools.partial(project_kernel, feeds=feeds, pairs=dets...  48.5 us
    pallas_call x1, Pallas kernels, back_project(): pl.pallas_call(functools.partial(back_kernel, feeds=feeds, pairs=dets //...  26.7 us
    pallas_call x1, Pallas kernels, reduce_step(): pl.pallas_call(reduce_kernel, name='reduce_step', out_shape=jax.ShapeDtyp...  12.2 us
    unnamed x5, local copies, waits for them, and re-layouts  8.13 us

profile of v3, /device:TPU:1, one launch (start us, length us, event | category | flops | bytes accessed | tf_op | source)
XLA Modules:
  0.0 164.1 jit_solution(11817182565857548737)
XLA Ops:
  0.6 0.0 copy-start
  0.6 1.3 broadcast_subtract_fusion.starts
  2.0 1.3 copy.11.counts
  3.3 0.0 copy-done
  3.3 1.0 fusion.8
  4.3 1.1 multiply_convert_fusion
  5.4 0.3 copy.10
  5.7 0.9 reshape.16.ids
  6.5 1.0 fusion.1
  7.6 48.5 %project.1.own = bf16[32,4,16,512]{3,2,1,0:T(8,128)(2,1)} custom-call(s32[4096]{0:T(1024)} %reshape.16.ids, bf16[16,8192]{1,0:T(8,128)(2,1)} %bitcast.5, bf16[128,64,256]{2,1,0:T(8,128)(2,1)} %tiles.1), custom_call_target="tpu_custom_call" | custom-call | tf_op jit(solution)/shard_map/project/pallas_call | solution.py:187
  56.1 62.2 %exit_gradient.1 = (f32[2,32,8,4,512]{4,3,2,1,0:T(4,128)}, bf16[32,4,16,512]{3,2,1,0:T(8,128)(2,1)}) custom-call(s32[4,4]{1,0:T(4,128)} %broadcast_subtract_fusion.starts, s32[4,1]{1,0:T(4,128)} %copy.11.counts, bf16[32,4,16,512]{3,2,1,0:T(8,128)(2,1)} %project.1.own, bf16[2,256,256]{2,1,0:T(8,128)(2,1)} %probe.1, bf16[4,4,256,256]{3,2,1,0:T(8,128)(2,1)} %amp.1, ...), custom_call_target="tpu_custom_call" | custom-call | tf_op jit(solution)/shard_map/exit_gradient/pallas_call | solution.py:408
  118.4 26.7 %back_project.1.share = bf16[4,16,8192]{2,1,0:T(8,128)(2,1)} custom-call(s32[4096]{0:T(1024)} %reshape.16.ids, bf16[32,4,16,512]{3,2,1,0:T(8,128)(2,1)} %get-tuple-element.4.grad, bf16[128,64,256]{2,1,0:T(8,128)(2,1)} %tiles.1), custom_call_target="tpu_custom_call" | custom-call | tf_op jit(solution)/shard_map/back_project/pallas_call | solution.py:501
  145.1 12.2 %reduce_step.1 = f32[16,8192]{1,0:T(8,128)} custom-call(bf16[4,16,8192]{2,1,0:T(8,128)(2,1)} %back_project.1.share, bf16[16,8192]{1,0:T(8,128)(2,1)} %bitcast.6), custom_call_target="tpu_custom_call" | custom-call | tf_op jit(solution)/shard_map/reduce_step/pallas_call | solution.py:591
  157.3 1.9 %copy.14 = f32[2,8,8192]{2,1,0:T(8,128)} copy(f32[2,8,8192]{2,1,0:T(8,128)} %bitcast.4) | data formatting | bytes 1048576
  159.1 4.9 %copy.15 = f32[2,256,4,512]{3,2,1,0:T(4,128)} copy(f32[2,256,4,512]{3,2,1,0:T(4,128)} %bitcast.3) | data formatting | bytes 8388608
  (1 shorter events, 0.0 us)
Async XLA Ops:
  0.6 2.7 %copy-start = (s32[128,32,4]{0,2,1:T(4,128)S(1)}, s32[128,32,4]{0,2,1:T(4,128)}, u32[]{:S(2)}) copy-start(s32[128,32,4]{0,2,1:T(4,128)} %param.9) | copy-start | bytes 196612

commit v4 on v3

--- a/solution.py
+++ b/solution.py
@@ -3,6 +3,7 @@
 
 import jax
 import jax.numpy as jnp
+import numpy as np
 from jax import lax
 from jax.experimental import pallas as pl
 from jax.experimental.pallas import tpu as pltpu
@@ -15,12 +16,14 @@
 
 
 def dft_tables(width):
-    index = jnp.arange(width, dtype=jnp.int32)
+    index = np.arange(width, dtype=np.int32)
     phase = index[:, None] * index[None, :] % width
-    turn = 2.0 * math.pi / width * phase.astype(f32)
-    cosine = (jnp.cos(turn) / math.sqrt(width)).astype(bf16)
-    sine_neg = (-jnp.sin(turn) / math.sqrt(width)).astype(bf16)
-    return (cosine, sine_neg)
+    turn = np.float32(2.0 * math.pi / width) * phase.astype(np.float32)
+    cosine = (np.cos(turn) / np.float32(math.sqrt(width))).astype(bf16)
+    sine_neg = (-np.sin(turn) / np.float32(math.sqrt(width))).astype(bf16)
+    fwd = np.block([[cosine, -sine_neg], [sine_neg, cosine]])
+    inv = np.block([[cosine, sine_neg], [-sine_neg, cosine]])
+    return jnp.asarray(fwd), jnp.asarray(inv)
 
 
 def low_half(shape):
@@ -128,6 +131,7 @@
     lo = low_half((rows, 128))
     half = pairs * rows
     lo_half = low_half((half, 128))
+    total = groups * angles
 
     def group_step(step, carry):
         @pl.when(step > 0)
@@ -136,12 +140,12 @@
 
         group = ang_peer(step, True)
         for a in range(angles):
-            at = (group * angles + a) * (2 * pairs * feeds)
+            at = group * angles + a
             halves = []
             for parity in range(2):
                 for bp in range(pairs):
-                    first = at + (2 * bp + parity) * feeds
-                    tile = [spread[ids[first + j]] for j in range(feeds)]
+                    first = (2 * bp + parity) * feeds
+                    tile = [spread[ids[(first + j) * total + at]] for j in range(feeds)]
                     halves.append(
                         jnp.concatenate(
                             [jnp.where(lo, tile[j], tile[j + 1]) for j in range(0, feeds, 2)],
@@ -241,19 +245,28 @@
             spill_out.at[a], spill_in.at[a], pos_send.at[1, a], pos_recv.at[1, a], {"pos": after}
         )
 
-    def outgoing(a, step):
+    parts = (slice(0, side), slice(side, tile_width))
+
+    def outgoing(a, h, step):
         group = ang_peer(step, True)
         return remote(
-            rounded.at[a, group], back.at[me, a], ang_send.at[a, step], ang_recv.at[a, step],
-            {"ang": group},
-        )
-
-    def incoming(a, step):
+            rounded.at[a, group, :, parts[h]], back.at[me, a, :, parts[h]],
+            ang_send.at[a, h, step], ang_recv.at[a, h, step], {"ang": group},
+        )
+
+    def incoming(a, h, step):
         group = ang_peer(step, False)
         return remote(
-            rounded.at[a, group], back.at[group, a], ang_send.at[a, step], ang_recv.at[a, step],
-            {"ang": group},
-        )
+            rounded.at[a, group, :, parts[h]], back.at[group, a, :, parts[h]],
+            ang_send.at[a, h, step], ang_recv.at[a, h, step], {"ang": group},
+        )
+
+    def depart(a, h):
+        def body(step, carry):
+            outgoing(a, h, step).start()
+            return carry
+
+        lax.fori_loop(0, groups - 1, body, 0)
 
     def keep(a):
         return pltpu.make_async_copy(rounded.at[a, me], back.at[me, a], own_sem.at[a])
@@ -292,7 +305,7 @@
             part = landed[a, :, :, lane * 128 : (lane + 1) * 128]
             strip[lane] = part.reshape(n, 128)
         for slot in range(slots):
-            start = starts[a, slot]
+            start = lax.rem(starts[a, slot], tile_width)
             block = lax.div(start, 128)
             shift = start - block * 128
             source = lax.broadcasted_iota(jnp.int32, (window, side), 0)
@@ -321,7 +334,7 @@
             near = jnp.dot(turned, fwd[...], preferred_element_type=f32)
             near_re = near[:, :side]
             near_im = near[:, side:]
-            live = jnp.minimum(jnp.maximum(counts[a, 0] - slot, 0), 1).astype(f32)
+            live = jnp.minimum(jnp.maximum(counts[a] - slot, 0), 1).astype(f32)
             grad_re = (probe_re * near_re + probe_im * near_im) * live
             grad_im = (probe_re * near_im - probe_im * near_re) * live
             both = jnp.concatenate(
@@ -332,12 +345,18 @@
                 axis=1,
             ).reshape(n, side)
             patches[:, slot * side : (slot + 1) * side] = both.astype(bf16)
+            if slot == slots - 2:
+
+                @pl.when(a > 0)
+                def _():
+                    send(a - 1)
+
         whole = tile_width + side
         source = lax.broadcasted_iota(jnp.int32, (side, whole), 1)
         target = lax.broadcasted_iota(jnp.int32, (side, whole), 0)
         place = jnp.concatenate(
             [
-                jnp.where(source - target == starts[a, slot], 1.0, 0.0).astype(bf16)
+                jnp.where(source - target == lax.rem(starts[a, slot], tile_width), 1.0, 0.0).astype(bf16)
                 for slot in range(slots)
             ],
             axis=0,
@@ -345,8 +364,12 @@
         over = jnp.dot(patches[...], place[:, tile_width:], preferred_element_type=f32)
         spill_out[a] = over.astype(bf16).reshape(groups, rows, side)
         inside = jnp.dot(patches[...], place[:, :tile_width], preferred_element_type=f32)
+        spill(a).start()
+        rounded[a, :, :, side:] = inside[:, side:].astype(bf16).reshape(
+            groups, rows, tile_width - side
+        )
         summed[a] = inside.reshape(groups, rows, tile_width)
-        spill(a).start()
+        depart(a, 1)
 
     def send(a):
         spill(a).wait_recv()
@@ -355,27 +378,16 @@
             left = summed[a, g, :, :side] + spill_in[a, g].astype(f32)
             summed[a, g, :, :side] = left
             rounded[a, g, :, :side] = left.astype(bf16)
-            rounded[a, g, :, side:] = summed[a, g, :, side:].astype(bf16)
             return carry
 
         lax.fori_loop(0, groups, body, 0, unroll=2)
         for c in range(2):
             store(a, c).start()
-
-        def depart(step, carry):
-            outgoing(a, step).start()
-            return carry
-
-        lax.fori_loop(0, groups - 1, depart, 0)
+        depart(a, 0)
         keep(a).start()
 
     def angle_step(a, carry):
         compute(a)
-
-        @pl.when(a > 0)
-        def _():
-            send(a - 1)
-
         return carry
 
     lax.fori_loop(0, angles, angle_step, 0)
@@ -389,8 +401,9 @@
 
     def finish(step, carry):
         for a in range(angles):
-            outgoing(a, step).wait_send()
-            incoming(a, step).wait_recv()
+            for h in range(2):
+                outgoing(a, h, step).wait_send()
+                incoming(a, h, step).wait_recv()
         return carry
 
     lax.fori_loop(0, groups - 1, finish, 0)
@@ -427,15 +440,19 @@
             dma((angles,)),
             dma((2, angles)),
             dma((2, angles)),
-            dma((angles, groups - 1)),
-            dma((angles, groups - 1)),
+            dma((angles, 2, groups - 1)),
+            dma((angles, 2, groups - 1)),
         ],
         compiler_params=pltpu.CompilerParams(collective_id=2, has_side_effects=True),
     )(starts, counts, own, probe, amp, fwd, inv)
 
 
-def back_kernel(ids, grad, tiles, out, *accs, feeds, pairs, angles):
+def back_kernel(ids, grad, tiles, exact, out, kept, *scratch, feeds, pairs, angles):
     step = pl.program_id(0)
+    accs = scratch[:-1]
+    total = pl.num_programs(0) * angles
+    keep = pltpu.make_async_copy(exact, kept.at[:, pl.ds(step, 1)], scratch[-1])
+    keep.start()
     owners, rows, width = out.shape
     blocks = accs[0].shape[0]
 
@@ -451,7 +468,7 @@
     half = pairs * rows
     lo = low_half((half, 128))
     for a in range(angles):
-        at = (step * angles + a) * (2 * pairs * feeds)
+        at = step * angles + a
         flat = jnp.concatenate(
             [grad[0, a, :, bp * 128 : (bp + 1) * 128] for bp in range(pairs)], axis=0
         )
@@ -461,13 +478,15 @@
         contrib = jnp.dot(halves, twice, preferred_element_type=f32)
         for parity in range(2):
             for bp in range(pairs):
-                first = at + (2 * bp + parity) * feeds
+                first = (2 * bp + parity) * feeds
                 top = (parity * pairs + bp) * rows
-                where = [ids[first + j] for j in range(feeds)]
+                where = [ids[(first + j) * total + at] for j in range(feeds)]
                 old = [accs[j][where[j]] for j in range(feeds)]
                 for j in range(feeds):
                     lane = j // 2 * 128
                     accs[j][where[j]] = old[j] + contrib[top : top + rows, lane : lane + 128]
+
+    keep.wait()
 
     @pl.when(step == pl.num_programs(0) - 1)
     def _():
@@ -491,7 +510,7 @@
         lax.fori_loop(0, per_owner, join, 0, unroll=2)
 
 
-def back_project(ids, grad, tiles, owners, coefs):
+def back_project(ids, grad, tiles, exact, owners, coefs):
     groups, angles, rows, tile_width = grad.shape
     angle_count, block, span = tiles.shape
     feeds = span // block
@@ -501,18 +520,26 @@
     return pl.pallas_call(
         functools.partial(back_kernel, feeds=feeds, pairs=dets // 2, angles=angles),
         name="back_project",
-        out_shape=jax.ShapeDtypeStruct((owners, rows, width), bf16),
+        out_shape=[
+            jax.ShapeDtypeStruct((owners, rows, width), bf16),
+            jax.ShapeDtypeStruct(exact.shape, f32),
+        ],
         grid_spec=pltpu.PrefetchScalarGridSpec(
             num_scalar_prefetch=1,
             grid=(groups,),
             in_specs=[
                 pl.BlockSpec((1, angles, rows, tile_width), lambda g, ids: (g, 0, 0, 0)),
                 pl.BlockSpec((angles, block, span), lambda g, ids: (g, 0, 0)),
+                pl.BlockSpec((2, 1, rows // 2, angles, tile_width), lambda g, ids: (0, g, 0, 0, 0)),
             ],
-            out_specs=pl.BlockSpec((owners, rows, width), lambda g, ids: (0, 0, 0)),
-            scratch_shapes=[pltpu.VMEM((blocks, rows, 128), f32) for _ in range(feeds)],
+            out_specs=[
+                pl.BlockSpec((owners, rows, width), lambda g, ids: (0, 0, 0)),
+                pl.BlockSpec(memory_space=pl.ANY),
+            ],
+            scratch_shapes=[pltpu.VMEM((blocks, rows, 128), f32) for _ in range(feeds)]
+            + [pltpu.SemaphoreType.DMA],
         ),
-    )(ids, grad, tiles)
+    )(ids, grad, tiles, exact)
 
 
 def reduce_kernel(share, vol, out, near, mixed, far, send, recv):
@@ -618,21 +645,14 @@
     rows = parts * slab
 
     held = volume.reshape(rows, width)
-    ids = lax.dynamic_slice_in_dim(tile_blocks, pos_index * own_blocks, own_blocks, 1).reshape(-1)
-    cosine, sine_neg = dft_tables(side)
-    fwd = jnp.concatenate(
-        [jnp.concatenate([cosine, -sine_neg], 1), jnp.concatenate([sine_neg, cosine], 1)], 0
-    )
-    inv = jnp.concatenate(
-        [jnp.concatenate([cosine, sine_neg], 1), jnp.concatenate([-sine_neg, cosine], 1)], 0
-    )
-    starts = offsets - pos_index * tile_width
-
+    by_angle = tile_blocks.transpose(1, 2, 0)
+    ids = lax.dynamic_slice_in_dim(by_angle, pos_index * own_blocks, own_blocks, 0).reshape(-1)
+    fwd, inv = dft_tables(side)
     own = project(ids, held, radon_tiles, n_ang, n_pos)
-    grad, back = exit_gradient(starts, counts, own, probe_field, amplitudes, fwd, inv)
-    share = back_project(ids, back, radon_tiles, n_pos, n_pos * width)
+    grad, back = exit_gradient(offsets, counts.reshape(-1), own, probe_field, amplitudes, fwd, inv)
+    share, kept = back_project(ids, back, radon_tiles, grad, n_pos, n_pos * width)
     new_volume = reduce_step(share, held).reshape(volume.shape)
-    proj_grad = grad.reshape(parts, n_ang * slab, angles, tile_width)
+    proj_grad = kept.reshape(parts, n_ang * slab, angles, tile_width)
     return (new_volume, proj_grad)
 
 

time: 165 us -> 162 us (0.982)
  Pallas kernels: 150 us -> 157 us
  local copies, waits for them, and re-layouts: 9.25 us -> 3.31 us
  other arithmetic: 4.45 us -> 0 us
    pallas_call x1, Pallas kernels: 26.7 us -> 33.5 us  [back_project(): pl.pallas_call(functools.partial(back_kernel, feeds=feeds, pairs=dets //...]
    unnamed x5 -> x3, local copies, waits for them, and re-layouts: 8.13 us -> 2.7 us
where the time goes in v4:
time: 162 us; the launch traced here: 161 us
  Pallas kernels  157 us (97%)
  local copies, waits for them, and re-layouts  3.31 us (2%)
    pallas_call x1, Pallas kernels, exit_gradient(): pl.pallas_call(functools.partial(exit_kernel, slots=slots, groups=groups,...  62.1 us
    pallas_call x1, Pallas kernels, project(): pl.pallas_call(functools.partial(project_kernel, feeds=feeds, pairs=dets...  48.6 us
    pallas_call x1, Pallas kernels, back_project(): pl.pallas_call(functools.partial(back_kernel, feeds=feeds, pairs=dets //...  33.5 us
    pallas_call x1, Pallas kernels, reduce_step(): pl.pallas_call(reduce_kernel, name='reduce_step', out_shape=jax.ShapeDtyp...  12.6 us

profile of v4, /device:TPU:1, one launch (start us, length us, event | category | flops | bytes accessed | tf_op | source)
XLA Modules:
  0.0 160.7 jit_solution(16200929036474806281)
XLA Ops:
  0.6 0.0 copy-start
  0.6 0.8 copy-done
  1.5 0.6 constant_dynamic-slice_fusion
  2.1 48.6 %project.1.own = bf16[32,4,16,512]{3,2,1,0:T(8,128)(2,1)} custom-call(s32[4096]{0:T(1024)} %bitcast.10, bf16[16,8192]{1,0:T(8,128)(2,1)} %bitcast.8, bf16[128,64,256]{2,1,0:T(8,128)(2,1)} %tiles.1), custom_call_target="tpu_custom_call" | custom-call | tf_op jit(solution)/shard_map/project/pallas_call | solution.py:191
  50.7 62.1 %exit_gradient.1 = (f32[2,32,8,4,512]{4,3,2,1,0:T(4,128)}, bf16[32,4,16,512]{3,2,1,0:T(8,128)(2,1)}) custom-call(s32[4,4]{1,0:T(4,128)} %starts.1, s32[4]{0:T(128)} %bitcast.12, bf16[32,4,16,512]{3,2,1,0:T(8,128)(2,1)} %project.1.own, bf16[2,256,256]{2,1,0:T(8,128)(2,1)} %probe.1, bf16[4,4,256,256]{3,2,1,0:T(8,128)(2,1)} %amp.1, ...), custom_call_target="tpu_custom_call" | custom-call | tf_op jit(solution)/shard_map/exit_gradient/pallas_call | solution.py:421
  112.8 33.5 %back_project.1 = (bf16[4,16,8192]{2,1,0:T(8,128)(2,1)}, f32[2,32,8,4,512]{4,3,2,1,0:T(4,128)}) custom-call(s32[4096]{0:T(1024)} %bitcast.11, bf16[32,4,16,512]{3,2,1,0:T(8,128)(2,1)} %get-tuple-element.6.grad, bf16[128,64,256]{2,1,0:T(8,128)(2,1)} %tiles.1, f32[2,32,8,4,512]{4,3,2,1,0:T(4,128)} %get-tuple-element.7.exact), custom_call_target="tpu_custom_call" | custom-call | tf_op jit(solution)/shard_map/back_project/pallas_call | solution.py:520
  146.3 12.6 %reduce_step.1 = f32[16,8192]{1,0:T(8,128)} custom-call(bf16[4,16,8192]{2,1,0:T(8,128)(2,1)} %get-tuple-element.8.share, bf16[16,8192]{1,0:T(8,128)(2,1)} %bitcast.9), custom_call_target="tpu_custom_call" | custom-call | tf_op jit(solution)/shard_map/reduce_step/pallas_call | solution.py:618
  158.9 1.9 %copy.12 = f32[2,8,8192]{2,1,0:T(8,128)} copy(f32[2,8,8192]{2,1,0:T(8,128)} %bitcast.7) | data formatting | bytes 1048576
Async XLA Ops:
  0.6 0.8 copy-start

commit v5 on v4

--- a/solution.py
+++ b/solution.py
@@ -449,10 +449,22 @@
 
 def back_kernel(ids, grad, tiles, exact, out, kept, *scratch, feeds, pairs, angles):
     step = pl.program_id(0)
-    accs = scratch[:-1]
-    total = pl.num_programs(0) * angles
-    keep = pltpu.make_async_copy(exact, kept.at[:, pl.ds(step, 1)], scratch[-1])
-    keep.start()
+    accs = scratch[:-2]
+    held, sem = scratch[-2:]
+    steps = pl.num_programs(0)
+    total = steps * angles
+    take = pltpu.make_async_copy(exact, held, sem.at[0])
+    give = pltpu.make_async_copy(held, kept, sem.at[1])
+
+    @pl.when(step == 0)
+    def _():
+        take.start()
+
+    @pl.when(step == steps // 2)
+    def _():
+        take.wait()
+        give.start()
+
     owners, rows, width = out.shape
     blocks = accs[0].shape[0]
 
@@ -486,10 +498,9 @@
                     lane = j // 2 * 128
                     accs[j][where[j]] = old[j] + contrib[top : top + rows, lane : lane + 128]
 
-    keep.wait()
-
-    @pl.when(step == pl.num_programs(0) - 1)
+    @pl.when(step == steps - 1)
     def _():
+        give.wait()
         lo = low_half((rows, 128))
         per_owner = width // 128
 
@@ -530,14 +541,14 @@
             in_specs=[
                 pl.BlockSpec((1, angles, rows, tile_width), lambda g, ids: (g, 0, 0, 0)),
                 pl.BlockSpec((angles, block, span), lambda g, ids: (g, 0, 0)),
-                pl.BlockSpec((2, 1, rows // 2, angles, tile_width), lambda g, ids: (0, g, 0, 0, 0)),
+                pl.BlockSpec(memory_space=pl.ANY),
             ],
             out_specs=[
                 pl.BlockSpec((owners, rows, width), lambda g, ids: (0, 0, 0)),
                 pl.BlockSpec(memory_space=pl.ANY),
             ],
             scratch_shapes=[pltpu.VMEM((blocks, rows, 128), f32) for _ in range(feeds)]
-            + [pltpu.SemaphoreType.DMA],
+            + [pltpu.VMEM(exact.shape, f32), pltpu.SemaphoreType.DMA((2,))],
         ),
     )(ids, grad, tiles, exact)
 

time: 162 us -> 155 us (0.957)
  Pallas kernels: 157 us -> 150 us
    pallas_call x1, Pallas kernels: 33.5 us -> 27.1 us  [back_project(): pl.pallas_call(functools.partial(back_kernel, feeds=feeds, pairs=dets //...]
where the time goes in v5:
time: 155 us; the launch traced here: 154 us
  Pallas kernels  150 us (97%)
  local copies, waits for them, and re-layouts  3.31 us (2%)
    pallas_call x1, Pallas kernels, exit_gradient(): pl.pallas_call(functools.partial(exit_kernel, slots=slots, groups=groups,...  62.1 us
    pallas_call x1, Pallas kernels, project(): pl.pallas_call(functools.partial(project_kernel, feeds=feeds, pairs=dets...  48.6 us
    pallas_call x1, Pallas kernels, back_project(): pl.pallas_call(functools.partial(back_kernel, feeds=feeds, pairs=dets //...  27.1 us
    pallas_call x1, Pallas kernels, reduce_step(): pl.pallas_call(reduce_kernel, name='reduce_step', out_shape=jax.ShapeDtyp...  12.6 us

profile of v5, /device:TPU:1, one launch (start us, length us, event | category | flops | bytes accessed | tf_op | source)
XLA Modules:
  0.0 154.4 jit_solution(1666346677458047198)
XLA Ops:
  0.6 0.0 copy-start
  0.6 0.8 copy-done
  1.5 0.6 constant_dynamic-slice_fusion
  2.1 48.6 %project.1.own = bf16[32,4,16,512]{3,2,1,0:T(8,128)(2,1)} custom-call(s32[4096]{0:T(1024)} %bitcast.10, bf16[16,8192]{1,0:T(8,128)(2,1)} %bitcast.8, bf16[128,64,256]{2,1,0:T(8,128)(2,1)} %tiles.1), custom_call_target="tpu_custom_call" | custom-call | tf_op jit(solution)/shard_map/project/pallas_call | solution.py:191
  50.7 62.1 %exit_gradient.1 = (f32[2,32,8,4,512]{4,3,2,1,0:T(4,128)}, bf16[32,4,16,512]{3,2,1,0:T(8,128)(2,1)}) custom-call(s32[4,4]{1,0:T(4,128)} %starts.1, s32[4]{0:T(128)} %bitcast.12, bf16[32,4,16,512]{3,2,1,0:T(8,128)(2,1)} %project.1.own, bf16[2,256,256]{2,1,0:T(8,128)(2,1)} %probe.1, bf16[4,4,256,256]{3,2,1,0:T(8,128)(2,1)} %amp.1, ...), custom_call_target="tpu_custom_call" | custom-call | tf_op jit(solution)/shard_map/exit_gradient/pallas_call | solution.py:421
  112.8 27.1 %back_project.1 = (bf16[4,16,8192]{2,1,0:T(8,128)(2,1)}, f32[2,32,8,4,512]{4,3,2,1,0:T(4,128)}) custom-call(s32[4096]{0:T(1024)} %bitcast.11, bf16[32,4,16,512]{3,2,1,0:T(8,128)(2,1)} %get-tuple-element.6.grad, bf16[128,64,256]{2,1,0:T(8,128)(2,1)} %tiles.1, f32[2,32,8,4,512]{4,3,2,1,0:T(4,128)} %get-tuple-element.7.exact), custom_call_target="tpu_custom_call" | custom-call | tf_op jit(solution)/shard_map/back_project/pallas_call | solution.py:531
  139.9 12.6 %reduce_step.1 = f32[16,8192]{1,0:T(8,128)} custom-call(bf16[4,16,8192]{2,1,0:T(8,128)(2,1)} %get-tuple-element.8.share, bf16[16,8192]{1,0:T(8,128)(2,1)} %bitcast.9), custom_call_target="tpu_custom_call" | custom-call | tf_op jit(solution)/shard_map/reduce_step/pallas_call | solution.py:629
  152.5 1.9 %copy.12 = f32[2,8,8192]{2,1,0:T(8,128)} copy(f32[2,8,8192]{2,1,0:T(8,128)} %bitcast.7) | data formatting | bytes 1048576
Async XLA Ops:
  0.6 0.8 copy-start
